TPU v7x, 32 devices: a whole 2x2x4 slice. The times are simulated.
32 devices in a mesh: expert: 32 (over z, y, x, core).
Axes of the slice: x: 2, y: 2, z: 4, core: 2. Of those that a mesh axis runs over, the one named last changes fastest.
Arguments:
- tokens: bfloat16 [4096, 1024], P('expert'), may hold values from -6 to 6
- gain_attend: bfloat16 [1024], P('expert'), may hold values from 0.5 to 1.5
- joint_weight: bfloat16 [1024, 3072], P('expert'), may hold values from -0.1875 to 0.1875
- merge_weight: bfloat16 [1024, 1024], P('expert'), may hold values from -0.5 to 0.5
- gain_feed: bfloat16 [1024], P('expert'), may hold values from 0.5 to 1.5
- up_weight: bfloat16 [1024, 4096], P('expert'), may hold values from -0.1875 to 0.1875
- down_weight: bfloat16 [4096, 1024], P('expert'), may hold values from -0.1875 to 0.1875
- router_weight: bfloat16 [1024, 32], P('expert'), may hold values from -0.12988281 to 0.12988281
- mix_weight: bfloat16 [1024, 2], P('expert'), may hold values from -0.1796875 to 0.1796875
- widen_weight: bfloat16 [32, 1024, 4096], P('expert'), may hold values from -0.1875 to 0.1875
- narrow_weight: bfloat16 [32, 4096, 1024], P('expert'), may hold values from -9.875 to 9.875
- routes: int32 [4096, 1], P('expert'), may hold values from 0 to 31; in each aligned block of 128 rows (0 to 127, 128 to 255, ...) at most 8 rows name the same one
- segments: int32 [32, 128], P('expert'), may hold values from 0 to 7, never falling along the last dimension, each value on 1 to 64 neighbouring positions
- cotangent: bfloat16 [4096, 1024], P('expert'), may hold values from -6 to 6
Outputs:
- result: bfloat16 [4096, 1024], P('expert')
- tokens_grad: bfloat16 [4096, 1024], P('expert')
- attend_grad: float32 [1024], P('expert')
- joint_grad: float32 [1024, 3072], P('expert')
- merge_grad: float32 [1024, 1024], P('expert')
- feed_grad: float32 [1024], P('expert')
- up_grad: float32 [1024, 4096], P('expert')
- down_grad: float32 [4096, 1024], P('expert')
- router_grad: float32 [1024, 32], P('expert')
- mix_grad: float32 [1024, 2], P('expert')
- widen_grad: float32 [32, 1024, 4096], P('expert')
- narrow_grad: float32 [32, 4096, 1024], P('expert')
Inputs may be any that keep to these rules, and one draw needn't show every extreme that they name: `routes`: no expert is named by more than 8 of the rows of one device; some expert is named by exactly 8 rows of one device. `segments`: along each sequence the numbers never fall; each document holds 1 to 64 positions, one exactly 64.
All inputs are finite; a program needn't handle non-finite values.
Results may differ from a plain program's by a relative error of at most 0.014.
Values may be sent and summed in bfloat16 or wider, within the bound.
No kernel may reach another device: no remote copies, remote signals or barrier semaphores. Data moves between devices by JAX's collectives and lax.ppermute only.
A program may use at most 192 MiB of HBM per device.

v0:
```python
import functools
import math

import jax
import jax.numpy as jnp
from jax import lax
from jax.experimental import pallas as pl
from jax.experimental.pallas import tpu as pltpu
from jax.sharding import PartitionSpec as P

HEAD_DIM = 64
TEAM = 8
EPSILON = 1e-05
HIDDEN = -1e30
F32 = jnp.float32
BF16 = jnp.bfloat16
CURVE = math.sqrt(2.0 / math.pi)
MIB = 1 << 20


def dot(left, right):
    return jnp.dot(left, right, preferred_element_type=F32)


def dot_tn(left, right):
    return lax.dot_general(left, right, (((0,), (0,)), ((), ())), preferred_element_type=F32)


def dot_nt(left, right):
    return lax.dot_general(left, right, (((1,), (1,)), ((), ())), preferred_element_type=F32)


def gelu_both(u):
    square = u * u
    bent = jnp.tanh(u * (CURVE + (CURVE * 0.044715) * square))
    half = 0.5 + 0.5 * bent
    slope = half + u * (1.0 - bent * bent) * (0.5 * CURVE + (0.5 * CURVE * 0.134145) * square)
    return u * half, slope


def normed(values):
    mean = jnp.mean(values, axis=-1, keepdims=True)
    centered = values - mean
    spread = jnp.mean(centered * centered, axis=-1, keepdims=True)
    scale = lax.rsqrt(spread + EPSILON)
    return centered * scale, scale


def norm_back(dn, unit, scale):
    return scale * (
        dn
        - jnp.mean(dn, axis=-1, keepdims=True)
        - unit * jnp.mean(dn * unit, axis=-1, keepdims=True)
    )


def lanes(shape):
    return lax.broadcasted_iota(jnp.int32, shape, 1)


def sublanes(shape):
    return lax.broadcasted_iota(jnp.int32, shape, 0)


def gain_rows(small, count):
    shape = (8, small.shape[1])
    pick = (lanes(shape) == sublanes(shape) + count + 2) & (sublanes(shape) < 2)
    return dot_nt(jnp.where(pick, 1.0, 0.0).astype(BF16), small)


def column_of(rows, lane, width):
    shape = (rows.shape[0], width)
    pick = jnp.where((lanes(shape) == lane) & (sublanes(shape) == 0), 1.0, 0.0).astype(BF16)
    return dot_tn(rows.astype(BF16), pick)


def visible(segment_row, length):
    shape = (length, length)
    row, column = sublanes(shape), lanes(shape)
    segment = jnp.sum(jnp.where(row == column, segment_row, 0.0), axis=1, keepdims=True)
    return (row >= column) & (segment == segment_row)


def chance_of(query, keys, allowed):
    scores = dot_nt(query, keys) * (1.0 / math.sqrt(HEAD_DIM))
    scores = jnp.where(allowed, scores, HIDDEN)
    grown = jnp.exp(scores - jnp.max(scores, axis=1, keepdims=True))
    return grown * (1.0 / jnp.sum(grown, axis=1, keepdims=True))


def params(mib=56, **more):
    return pltpu.CompilerParams(vmem_limit_bytes=mib * MIB, **more)


def cost(flops=1):
    return pl.CostEstimate(flops=flops, bytes_accessed=1, transcendentals=0)


def shaped(dtype, *shape):
    return jax.ShapeDtypeStruct(shape, dtype)


def pack_kernel(
    joint_ref, up_ref, router_ref, mix_ref, gain_a_ref, gain_f_ref, pack_ref, *, teams
):
    rows = joint_ref.shape[0]
    width = joint_ref.shape[1] // 3
    part = width // TEAM
    block = up_ref.shape[1] // (teams * TEAM)
    count = router_ref.shape[1]
    wide = pack_ref.shape[2] - teams * block
    shape = (rows, wide - 3 * part)
    spread = (count, shape[1])
    spread = jnp.where(lanes(spread) == sublanes(spread), 1.0, 0.0).astype(BF16)
    small = dot(router_ref[...], spread)
    lane = lanes(shape)
    square = (rows, rows)
    same = sublanes(square) == lanes(square)
    columns = [mix_ref[0:1], mix_ref[1:2], gain_a_ref[...], gain_f_ref[...]]
    for i, row in enumerate(columns):
        column = jnp.sum(jnp.where(same, row.astype(F32), 0.0), axis=1, keepdims=True)
        small += jnp.where(lane == count + i, column, 0.0)
    small = small.astype(BF16)
    for p in range(TEAM):
        pieces = [joint_ref[:, c * width + p * part : c * width + (p + 1) * part] for c in range(3)]
        for g in range(teams):
            start = (g * TEAM + p) * block
            pieces.append(up_ref[:, start : start + block])
        pack_ref[p] = jnp.concatenate(pieces[:3] + [small] + pieces[3:], axis=1)


def attend_kernel(place_ref, n0_ref, n1_ref, f0_ref, f1_ref, got_ref, joint_ref, out_ref, *, count):
    _, length, part = out_ref.shape
    members = [ref.at[i] for ref in (n0_ref, n1_ref, f0_ref, f1_ref) for i in range(2)]
    gains = gain_rows(got_ref[:, 3 * part :], count)
    lane = lanes((length, part))
    for j in range(TEAM // 2):
        pair = (members[j], members[j + TEAM // 2])
        x = jnp.concatenate([ref[:length] for ref in pair], axis=0).astype(F32)
        unit, _ = normed(x)
        first = (unit * gains[0:1]).astype(BF16)
        joint = dot(first, got_ref[:, : 3 * part]).astype(BF16)
        for k, ref in enumerate(pair):
            allowed = visible(ref[length:, :length].astype(F32)[0:1], length)
            own = joint[k * length : (k + 1) * length]
            query, keys, values = own[:, :part], own[:, part : 2 * part], own[:, 2 * part :]
            total = jnp.zeros((length, part), F32)
            for h in range(part // HEAD_DIM):
                mine = lane // HEAD_DIM == h
                chance = chance_of(jnp.where(mine, query, 0), keys, allowed)
                total += dot(chance.astype(BF16), jnp.where(mine, values, 0))
            member = place_ref[0] ^ (2 * j + k)
            joint_ref[member] = own
            out_ref[member] = total.astype(BF16)


def attend(place, xs, got, length, count):
    part = xs[0].shape[2] // TEAM
    return pl.pallas_call(
        functools.partial(attend_kernel, count=count),
        in_specs=[pl.BlockSpec(memory_space=pltpu.SMEM)]
        + [pl.BlockSpec(memory_space=pltpu.VMEM)] * 5,
        out_shape=(shaped(BF16, TEAM, length, 3 * part), shaped(BF16, TEAM, length, part)),
        compiler_params=params(56),
        cost_estimate=cost(),
        name="attend",
    )(place, *xs, got)


def attend_back_kernel(
    place_ref, n0_ref, n1_ref, f0_ref, f1_ref, near_att, far_att, got_ref, joint_ref, d_ref, side_ref,
    keep_ref, send_ref, grad_ref, d_joint_ref, first_ref, unit_ref, d_merged_ref, *, count,
):
    _, length, wide = joint_ref.shape
    part = wide // 3
    half, _, width = near_att.shape
    shrink = 1.0 / math.sqrt(HEAD_DIM)
    gains = gain_rows(got_ref[:, 3 * part :], count)
    lane = lanes((length, part))

    def step(i, carry, start, k, ref):
        j = start + i
        rows = pl.ds(pl.multiple_of((k * half + j) * length, length), length)
        x = ref[i]
        unit, _ = normed(x[:length].astype(F32))
        unit_ref[rows] = unit
        first_ref[rows] = (unit * gains[0:1]).astype(BF16)
        allowed = visible(x[length:, :length].astype(F32)[0:1], length)
        member = place_ref[0] ^ (2 * j + k)
        own = joint_ref[member]
        both = d_ref[member]
        d_own = both[:length]
        d_merged_ref[rows] = both[length:]
        query, keys, values = own[:, :part], own[:, part : 2 * part], own[:, 2 * part :]
        d_query = jnp.zeros((length, part), F32)
        d_keys = jnp.zeros((length, part), F32)
        d_values = jnp.zeros((length, part), F32)
        for h in range(part // HEAD_DIM):
            mine = lane // HEAD_DIM == h
            q = jnp.where(mine, query, 0)
            d_head = jnp.where(mine, d_own, 0)
            chance = chance_of(q, keys, allowed)
            d_weights = dot_nt(d_head, values)
            inner = jnp.sum(chance * d_weights, axis=1, keepdims=True)
            d_scores = (chance * (d_weights - inner)).astype(BF16)
            d_query += dot(d_scores, jnp.where(mine, keys, 0))
            d_keys += dot_tn(d_scores, q)
            d_values += dot_tn(chance.astype(BF16), d_head)
        d_joint_ref[rows, :part] = (d_query * shrink).astype(BF16)
        d_joint_ref[rows, part : 2 * part] = (d_keys * shrink).astype(BF16)
        d_joint_ref[rows, 2 * part :] = d_values.astype(BF16)
        return carry

    for k, pair in enumerate(((n0_ref, n1_ref), (f0_ref, f1_ref))):
        for a, ref in enumerate(pair):
            lax.fori_loop(0, 2, functools.partial(step, start=2 * a, k=k, ref=ref), 0)
    d_joint = d_joint_ref[...]
    d_first = dot_nt(d_joint, got_ref[:, : 3 * part])
    tall = half * length
    keep_ref[...] = d_first[:tall].reshape(keep_ref.shape)
    send_ref[...] = d_first[tall:].astype(BF16).reshape(send_ref.shape)
    gain = jnp.sum(d_first * unit_ref[...], axis=0, keepdims=True)
    gain = jnp.where(sublanes((8, width)) == 0, gain, 0.0)
    grad_ref[:, : 3 * part] = dot_tn(first_ref[...], d_joint).astype(BF16)
    side = side_ref[...] + column_of(gain, count + 3, side_ref.shape[1])
    grad_ref[:, 3 * part : -part] = side.astype(BF16)
    d_merged = d_merged_ref[...]
    merged = dot_tn(near_att[...].reshape(tall, width), d_merged[:tall])
    merged += dot_tn(far_att[...].reshape(tall, width), d_merged[tall:])
    grad_ref[:, -part:] = merged.astype(BF16)


def attend_back(place, xs, near_att, far_att, got, joint, d_both, side, count):
    half, length, width = near_att.shape
    part = width // TEAM
    tall = TEAM * length
    outs = (
        shaped(F32, half, length, width),
        shaped(BF16, half, length, width),
        shaped(BF16, width, 4 * part + side.shape[1]),
    )
    return pl.pallas_call(
        functools.partial(attend_back_kernel, count=count),
        in_specs=[pl.BlockSpec(memory_space=pltpu.SMEM)]
        + [pl.BlockSpec(memory_space=pltpu.VMEM)] * 10,
        out_shape=outs,
        scratch_shapes=[
            pltpu.VMEM((tall, 3 * part), BF16),
            pltpu.VMEM((tall, width), BF16),
            pltpu.VMEM((tall, width), F32),
            pltpu.VMEM((tall, part), BF16),
        ],
        compiler_params=params(56),
        cost_estimate=cost(int(2e10)),
        name="attend_back",
    )(place, *xs, near_att, far_att, got, joint, d_both, side)


def middle_kernel(
    att_ref, merge_ref, x_ref, small_ref, routes_ref, placing_ref,
    residual_ref, second_ref, attended_ref, stats_ref, out_ref, *, count,
):
    length, width = x_ref.shape
    small = small_ref[:, 3 * width // TEAM :]
    gains = gain_rows(small, count)
    attended = jnp.concatenate([att_ref[p] for p in range(TEAM)], axis=1)
    residual = x_ref[...].astype(F32) + dot(attended, merge_ref[...])
    residual_ref[...] = residual
    unit, _ = normed(residual)
    second = (unit * gains[1:2]).astype(BF16)
    second_ref[...] = second
    attended_ref[...] = attended
    logits = dot(second, small)
    lane = lanes(logits.shape)
    routed = jnp.where(lane < count, logits, HIDDEN)
    grown = jnp.exp(routed - jnp.max(routed, axis=1, keepdims=True))
    chances = grown * (1.0 / jnp.sum(grown, axis=1, keepdims=True))
    mixed = jnp.where((lane >= count) & (lane < count + 2), logits, HIDDEN)
    grown = jnp.exp(mixed - jnp.max(mixed, axis=1, keepdims=True))
    mix = grown * (1.0 / jnp.sum(grown, axis=1, keepdims=True))
    routes = routes_ref[...]
    onehot = lane == routes
    gate = jnp.sum(jnp.where(onehot, chances, 0.0), axis=1, keepdims=True)
    mix_expert = jnp.sum(jnp.where(lane == count + 1, mix, 0.0), axis=1, keepdims=True)
    stats_ref[...] = chances + mix + jnp.where(lane == count + 2, gate, 0.0)
    scale = mix_expert * gate
    high = scale.astype(BF16).astype(F32)
    middle_part = (scale - high).astype(BF16).astype(F32)
    low = scale - high - middle_part
    spread = (length, out_ref.shape[1] - width)
    lane = lanes(spread)
    scales = jnp.where(lane == 0, high, 0.0) + jnp.where(lane == 1, middle_part, 0.0)
    scales += jnp.where(lane == 2, low, 0.0)
    placing = placing_ref[...]
    out_ref[:, :width] = dot_tn(placing, second).astype(BF16)
    out_ref[:, width:] = dot_tn(placing, scales.astype(BF16)).astype(BF16)


def place_kernel(routes_ref, g_ref, placing_ref, out_ref, *, count, capacity):
    length = g_ref.shape[0]
    routes = routes_ref[...]
    onehot = jnp.where(lanes((length, -(-count // 128) * 128)) == routes, 1.0, 0.0)
    shape = (length, length)
    before = jnp.where(sublanes(shape) > lanes(shape), 1.0, 0.0).astype(BF16)
    rank = jnp.sum(onehot * dot(before, onehot.astype(BF16)), axis=1, keepdims=True)
    slot = routes * capacity + rank.astype(jnp.int32)
    placing = jnp.where(lanes((length, count * capacity)) == slot, 1.0, 0.0).astype(BF16)
    placing_ref[...] = placing
    out_ref[...] = dot_tn(placing, g_ref[...]).astype(BF16)


def place_rows(routes, cotangent, count, capacity):
    length, width = cotangent.shape
    return pl.pallas_call(
        functools.partial(place_kernel, count=count, capacity=capacity),
        out_shape=(
            shaped(BF16, length, count * capacity),
            shaped(BF16, count * capacity, width),
        ),
        compiler_params=params(56),
        cost_estimate=cost(),
        name="place_rows",
    )(routes, cotangent)


def middle(att, merge, tokens, got, routes, placing, count):
    length, width = tokens.shape
    lanes_small = got.shape[1] - 3 * width // TEAM
    outs = (
        shaped(F32, length, width),
        shaped(BF16, length, width),
        shaped(BF16, length, width),
        shaped(F32, length, lanes_small),
        shaped(BF16, placing.shape[1], width + 128),
    )
    return pl.pallas_call(
        functools.partial(middle_kernel, count=count),
        out_shape=outs,
        compiler_params=params(56),
        cost_estimate=cost(),
        name="middle",
    )(att, merge, tokens, got, routes, placing)


def expert_kernel(
    rows_ref, g_ref, widen_hbm, narrow_hbm, act_hbm, d_hbm, back_ref, d_out_ref,
    widen_ref, narrow_ref, act_ref, d_ref, in_sems, out_sems, *, chunk,
):
    width, hidden = widen_ref.shape
    copies = []
    for i in range(hidden // chunk):
        part = pl.ds(i * chunk, chunk)
        wide = (widen_hbm.at[0, :, part], widen_ref.at[:, part], in_sems.at[2 * i])
        tall = (narrow_hbm.at[0, part, :], narrow_ref.at[part, :], in_sems.at[2 * i + 1])
        copies.append([pltpu.make_async_copy(*wide), pltpu.make_async_copy(*tall)])
    for pair in copies:
        for copy in pair:
            copy.start()
    scale = jnp.sum(rows_ref[:, width:].astype(F32), axis=1, keepdims=True)
    d_out_ref[...] = (g_ref[...].astype(F32) * scale).astype(BF16)

    def step(i, carry):
        part = pl.ds(pl.multiple_of(i * chunk, chunk), chunk)
        wide = (widen_hbm.at[0, :, part], widen_ref.at[:, part], in_sems.at[2 * i])
        tall = (narrow_hbm.at[0, part, :], narrow_ref.at[part, :], in_sems.at[2 * i + 1])
        pltpu.make_async_copy(*wide).wait()
        pltpu.make_async_copy(*tall).wait()
        upper = dot(rows_ref[:, :width], widen_ref[:, part])
        d_act = dot_nt(d_out_ref[...], narrow_ref[part])
        act, slope = gelu_both(upper)
        act_ref[:, part] = act.astype(BF16)
        d_ref[:, part] = (slope * d_act).astype(BF16)
        return carry

    lax.fori_loop(0, hidden // chunk, step, 0)
    outs = [
        pltpu.make_async_copy(act_ref, act_hbm, out_sems.at[0]),
        pltpu.make_async_copy(d_ref, d_hbm, out_sems.at[1]),
    ]
    for copy in outs:
        copy.start()
    half = width // 4

    def finish(i, carry):
        here, there = [pl.ds(pl.multiple_of(j, half), half) for j in (i * half, width + i * half)]
        back_ref[:, here] = dot(act_ref[...], narrow_ref[:, here]).astype(BF16)
        back_ref[:, there] = dot_nt(d_ref[...], widen_ref[here]).astype(BF16)
        return carry

    lax.fori_loop(0, 4, finish, 0)
    for copy in outs:
        copy.wait()


def expert(rows, g_rows, widen, narrow, chunk=512):
    slots, width = g_rows.shape
    hidden = widen.shape[2]
    left = pl.BlockSpec(memory_space=pl.ANY)
    here = pl.BlockSpec(memory_space=pltpu.VMEM)
    return pl.pallas_call(
        functools.partial(expert_kernel, chunk=chunk),
        in_specs=[here, here, left, left],
        out_specs=[left, left, here, here],
        out_shape=(
            shaped(BF16, slots, hidden),
            shaped(BF16, slots, hidden),
            shaped(BF16, slots, 2 * width),
            shaped(BF16, slots, width),
        ),
        scratch_shapes=[
            pltpu.VMEM((width, hidden), BF16),
            pltpu.VMEM((hidden, width), BF16),
            pltpu.VMEM((slots, hidden), BF16),
            pltpu.VMEM((slots, hidden), BF16),
            pltpu.SemaphoreType.DMA((2 * (hidden // chunk),)),
            pltpu.SemaphoreType.DMA((2,)),
        ],
        compiler_params=params(56),
        cost_estimate=cost(),
        name="expert",
    )(rows, g_rows, widen, narrow)


def narrow_grad_kernel(rows_ref, act_ref, out_ref):
    out_ref[0] = dot_tn(act_ref[...], rows_ref[...])


def narrow_grads(rows, act, chunk=512):
    slots, width = rows.shape
    hidden = act.shape[1]
    return pl.pallas_call(
        narrow_grad_kernel,
        grid=(hidden // chunk,),
        in_specs=[
            pl.BlockSpec((slots, width), lambda f: (0, 0)),
            pl.BlockSpec((slots, chunk), lambda f: (0, f)),
        ],
        out_specs=pl.BlockSpec((1, chunk, width), lambda f: (0, f, 0)),
        out_shape=shaped(F32, 1, hidden, width),
        compiler_params=params(56),
        cost_estimate=cost(),
        name="narrow_grads",
    )(rows, act)


def widen_grad_kernel(rows_ref, d_ref, out_ref):
    out_ref[0] = dot_tn(rows_ref[...], d_ref[...])


def widen_grads(rows, d_upper, width, chunk=128):
    slots = rows.shape[0]
    hidden = d_upper.shape[1]
    return pl.pallas_call(
        widen_grad_kernel,
        grid=(width // chunk,),
        in_specs=[
            pl.BlockSpec((slots, chunk), lambda f: (0, f)),
            pl.BlockSpec((slots, hidden), lambda f: (0, 0)),
        ],
        out_specs=pl.BlockSpec((1, chunk, hidden), lambda f: (0, f, 0)),
        out_shape=shaped(F32, 1, width, hidden),
        compiler_params=params(56),
        cost_estimate=cost(),
        name="widen_grads",
    )(rows, d_upper)


def feed_kernel(
    near_ref, far_ref, g_near_ref, g_far_ref, up_ref, down_ref, small_ref,
    keep_ref, low_ref, high_ref, keep_dense_ref, send_dense_ref, up_grad_ref, down_grad_ref,
    *, count,
):
    half, length, width = near_ref.shape
    tall = half * length
    near, far = near_ref[...].reshape(tall, width), far_ref[...].reshape(tall, width)
    second = jnp.concatenate([near, far], axis=0)
    g = jnp.concatenate(
        [g_near_ref[...].reshape(tall, width), g_far_ref[...].reshape(tall, width)], axis=0
    ).astype(F32)
    logits = dot(second, small_ref[:, 3 * width // TEAM :])
    lane = lanes(logits.shape)
    mixed = jnp.where((lane >= count) & (lane < count + 2), logits, HIDDEN)
    grown = jnp.exp(mixed - jnp.max(mixed, axis=1, keepdims=True))
    mix = jnp.sum(jnp.where(lane == count, grown, 0.0), axis=1, keepdims=True)
    mix = mix * (1.0 / jnp.sum(grown, axis=1, keepdims=True))
    d_dense = (g * mix).astype(BF16)
    act, slope = gelu_both(dot(second, up_ref[...]))
    act = act.astype(BF16)
    d_upper = (slope * dot_nt(d_dense, down_ref[...])).astype(BF16)
    d_second = dot_nt(d_upper, up_ref[...])
    dense = dot(act, down_ref[...])
    along = jnp.sum(g * dense, axis=1, keepdims=True)
    rest = along - along.astype(BF16).astype(F32)
    lane = lanes((2 * tall, 128))
    along = jnp.where(lane == 0, along, 0.0) + jnp.where(lane == 1, rest, 0.0)
    keep_ref[:, :, :width] = d_second[:tall].reshape(half, length, width)
    keep_ref[:, :, width:] = along[:tall].reshape(half, length, 128)
    sent = d_second[tall:].astype(BF16).reshape(half, length, width)
    low_ref[...] = sent[:, :, : width // 2]
    high_ref[:, :, : width // 2] = sent[:, :, width // 2 :]
    high_ref[:, :, width // 2 :] = along[tall:].astype(BF16).reshape(half, length, 128)
    keep_dense_ref[...] = dense[:tall].reshape(half, length, width)
    send_dense_ref[...] = dense[tall:].astype(BF16).reshape(half, length, width)
    up_grad_ref[...] = dot_tn(second, d_upper).astype(BF16)
    down_grad_ref[...] = dot_tn(act, d_dense).astype(BF16)


def feed(near, far, g_near, g_far, up, down, got, count):
    half, length, width = near.shape
    hidden = up.shape[1]
    outs = (
        shaped(F32, half, length, width + 128),
        shaped(BF16, half, length, width // 2),
        shaped(BF16, half, length, width // 2 + 128),
        shaped(F32, half, length, width),
        shaped(BF16, half, length, width),
        shaped(BF16, width, hidden),
        shaped(BF16, hidden, width),
    )
    return pl.pallas_call(
        functools.partial(feed_kernel, count=count),
        out_shape=outs,
        compiler_params=params(56),
        cost_estimate=cost(),
        name="feed",
    )(near, far, g_near, g_far, up, down, got)


def halve_kernel(keep_ref, *refs, pieces):
    got_refs, own_ref, send_refs = refs[:pieces], refs[pieces], refs[pieces + 1 :]
    size = 16

    def step(i, carry):
        rows = pl.ds(pl.multiple_of(i * size, size), size)
        start = 0
        for got_ref in got_refs:
            part = slice(start, start + got_ref.shape[2])
            own_ref[rows, part] = keep_ref[0, rows, part] + got_ref[0, rows].astype(F32)
            for j, ref in enumerate(send_refs):
                total = keep_ref[j + 1, rows, part] + got_ref[j + 1, rows].astype(F32)
                ref[rows, part] = total.astype(BF16)
            start = part.stop
        return carry

    lax.fori_loop(0, own_ref.shape[0] // size, step, 0)


def halve(keep, got):
    half, length, width = keep.shape
    outs = (shaped(F32, length, width),) + (shaped(BF16, length, width),) * (half - 1)
    return pl.pallas_call(
        functools.partial(halve_kernel, pieces=len(got)),
        out_shape=outs,
        compiler_params=params(20),
        cost_estimate=cost(),
        name="halve",
    )(keep, *got)


def after_kernel(
    own_ref, r1_ref, r2_ref, r3_ref, back_ref, placing_ref, residual_ref, stats_ref, g_ref,
    small_ref, merge_ref, routes_ref, second_ref,
    result_ref, d_residual_ref, side_ref, d_ref, *, count,
):
    length, width = g_ref.shape
    part = width // TEAM
    small = small_ref[:, 3 * part :]
    gains = gain_rows(small, count)
    summed = (
        own_ref[...] + r1_ref[...].astype(F32) + r2_ref[...].astype(F32) + r3_ref[...].astype(F32)
    )
    d_second = summed[:, :width]
    d_mix_dense = jnp.sum(summed[:, width:], axis=1, keepdims=True)
    stats = stats_ref[...]
    lane = lanes(stats.shape)
    column = lambda i: jnp.sum(jnp.where(lane == i, stats, 0.0), axis=1, keepdims=True)
    mix_dense, mix_expert, gate = column(count), column(count + 1), column(count + 2)
    residual = residual_ref[...]
    g = g_ref[...].astype(F32)
    returned = dot(placing_ref[...], back_ref[:, :width])
    result_ref[...] = residual + mix_expert * gate * returned
    along = jnp.sum(g * returned, axis=1, keepdims=True)
    d_mix_expert = gate * along
    mean = mix_dense * d_mix_dense + mix_expert * d_mix_expert
    onehot = jnp.where(lane == routes_ref[...], 1.0, 0.0)
    side = jnp.where(lane < count, stats * (onehot - gate) * (mix_expert * along), 0.0)
    side += jnp.where(lane == count, mix_dense * (d_mix_dense - mean), 0.0)
    side += jnp.where(lane == count + 1, mix_expert * (d_mix_expert - mean), 0.0)
    side = side.astype(BF16)
    d_second += dot(placing_ref[...], back_ref[:, width:]) + dot_nt(side, small)
    unit, scale = normed(residual)
    d_residual = g + norm_back(d_second * gains[1:2], unit, scale)
    d_residual_ref[...] = d_residual
    d_merged = d_residual.astype(BF16)
    side_grad = dot_tn(second_ref[...], side)
    feed_row = jnp.sum(d_second * unit, axis=0, keepdims=True)
    feed_rows = jnp.where(sublanes((8, width)) == 0, feed_row, 0.0)
    side_ref[...] = side_grad + column_of(feed_rows, count + 2, side.shape[1])
    d_att = dot_nt(d_merged, merge_ref[...]).astype(BF16)
    for p in range(TEAM):
        d_ref[p, :length] = d_att[:, p * part : (p + 1) * part]
        d_ref[p, length:] = d_merged[:, p * part : (p + 1) * part]


def after(
    own, others, back, placing, residual, stats, cotangent, got, merge, routes, second, count
):
    length, width = cotangent.shape
    part = width // TEAM
    outs = (
        shaped(F32, length, width),
        shaped(F32, length, width),
        shaped(F32, width, got.shape[1] - 3 * part),
        shaped(BF16, TEAM, 2 * length, part),
    )
    return pl.pallas_call(
        functools.partial(after_kernel, count=count),
        out_shape=outs,
        compiler_params=params(56),
        cost_estimate=cost(),
        name="after",
    )(own, *others, back, placing, residual, stats, cotangent, got, merge, routes, second)


def last_kernel(
    own_ref, r1_ref, r2_ref, r3_ref, dense_ref, d1_ref, d2_ref, d3_ref, part_ref, stats_ref,
    x_ref, d_residual_ref, small_ref, out_ref, result_ref, *, count,
):
    part = x_ref.shape[1] // TEAM
    gains = gain_rows(small_ref[:, 3 * part :], count)
    size = 32

    def step(i, carry):
        rows = pl.ds(pl.multiple_of(i * size, size), size)
        add = lambda own, *others: own[rows] + sum(ref[rows].astype(F32) for ref in others)
        d_first = add(own_ref, r1_ref, r2_ref, r3_ref)
        unit, scale = normed(x_ref[rows].astype(F32))
        out_ref[rows] = (
            d_residual_ref[rows] + norm_back(d_first * gains[0:1], unit, scale)
        ).astype(BF16)
        stats = stats_ref[rows]
        picked = jnp.where(lanes(stats.shape) == count, stats, 0.0)
        mix_dense = jnp.sum(picked, axis=1, keepdims=True)
        dense = add(dense_ref, d1_ref, d2_ref, d3_ref)
        result_ref[rows] = (part_ref[rows] + mix_dense * dense).astype(BF16)
        return carry

    lax.fori_loop(0, x_ref.shape[0] // size, step, 0)


def last(own, others, dense, more, part, stats, tokens, d_residual, got, count):
    return pl.pallas_call(
        functools.partial(last_kernel, count=count),
        out_shape=(shaped(BF16, *tokens.shape),) * 2,
        compiler_params=params(16),
        cost_estimate=cost(),
        name="last",
    )(own, *others, dense, *more, part, stats, tokens, d_residual, got)


def owner_kernel(
    got_ref, up_got_ref, joint_ref, merge_ref, up_ref, attend_ref, feed_ref, router_ref, mix_ref,
    *, count,
):
    teams, _, rows, wide = got_ref.shape
    part = merge_ref.shape[1] // TEAM
    width = part * TEAM
    block = up_ref.shape[1] // (TEAM * teams)

    def step(p, total):
        own = got_ref[0, p].astype(F32)
        for g in range(1, teams):
            own += got_ref[g, p].astype(F32)
        for c in range(3):
            start = pl.multiple_of(c * width + p * part, part)
            joint_ref[:, pl.ds(start, part)] = own[:, c * part : (c + 1) * part]
        merge_ref[:, pl.ds(pl.multiple_of(p * part, part), part)] = own[:, wide - part :]
        return total + own[:, 3 * part : wide - part]

    total = lax.fori_loop(0, TEAM, step, jnp.zeros((rows, wide - 4 * part), F32))
    for p in range(TEAM):
        for g in range(teams):
            start = (g * TEAM + p) * block
            piece = up_got_ref[p, :, g * block : (g + 1) * block]
            up_ref[:, start : start + block] = piece.astype(F32)
    router_ref[...] = total[:, :count]
    same = sublanes((rows, rows)) == lanes((rows, rows))

    def row(lane):
        column = jnp.sum(jnp.where(lanes(total.shape) == lane, total, 0.0), axis=1, keepdims=True)
        return jnp.sum(jnp.where(same, column, 0.0), axis=0, keepdims=True)

    mix_ref[0:1] = row(count)
    mix_ref[1:2] = row(count + 1)
    feed_ref[...] = row(count + 2)
    attend_ref[...] = row(count + 3)


def owner_sums(got, up, width, hidden, count):
    rows = got.shape[2]
    outs = (
        shaped(F32, rows, 3 * width),
        shaped(F32, rows, width),
        shaped(F32, rows, hidden),
        shaped(F32, 1, rows),
        shaped(F32, 1, rows),
        shaped(F32, rows, count),
        shaped(F32, 2, rows),
    )
    return pl.pallas_call(
        functools.partial(owner_kernel, count=count),
        out_shape=outs,
        compiler_params=params(12),
        cost_estimate=cost(),
        name="owner_sums",
    )(got, up)


def order_kernel(place_ref, near_ref, far_ref, out_ref):
    teams, _, rows, _ = out_ref.shape

    def step(j, carry):
        for k, ref in enumerate((near_ref, far_ref)):
            for d in range(teams):
                team = (place_ref[1] + d) & (teams - 1)
                out_ref[team, place_ref[0] ^ (2 * j + k)] = ref[j, d * rows : (d + 1) * rows]
        return carry

    lax.fori_loop(0, TEAM // 2, step, 0)


def order(place, near, far, teams):
    _, tall, width = near.shape
    out = shaped(BF16, teams, TEAM, tall // teams, width)
    return pl.pallas_call(
        order_kernel,
        in_specs=[pl.BlockSpec(memory_space=pltpu.SMEM)]
        + [pl.BlockSpec(memory_space=pltpu.VMEM)] * 2,
        out_shape=out,
        compiler_params=params(56),
        cost_estimate=cost(),
        name="order",
    )(place, near, far)


def body(
    tokens,
    gain_attend,
    joint_weight,
    merge_weight,
    gain_feed,
    up_weight,
    down_weight,
    router_weight,
    mix_weight,
    widen_weight,
    narrow_weight,
    routes,
    segments,
    cotangent,
):
    count = lax.axis_size("expert")
    teams = count // TEAM
    place = (lax.axis_index("expert") & (TEAM - 1)).astype(jnp.int32)
    team = lax.axis_index("expert") >> 3
    place_arg = jnp.stack([place, team.astype(jnp.int32)])
    length, width = tokens.shape
    capacity = max(2, 2 * length // count)
    planes = [[g * TEAM + p for p in range(TEAM)] for g in range(teams)]
    lines = [[g * TEAM + p for g in range(teams)] for p in range(TEAM)]
    rows = joint_weight.shape[0]
    part = width // TEAM
    hidden = up_weight.shape[1]
    block = hidden // count

    def swap(value, mask):
        return lax.ppermute(value, "expert", [(i, i ^ mask) for i in range(count)])

    def exchange(value):
        return lax.all_to_all(value, "expert", 0, 0, tiled=True)

    def team_exchange(value):
        return lax.all_to_all(value, "expert", 0, 0, tiled=True, axis_index_groups=planes)

    def line_gather(value):
        return lax.all_gather(value, "expert", axis=0, tiled=True, axis_index_groups=lines)

    def line_scatter(value):
        return lax.psum_scatter(
            value, "expert", scatter_dimension=0, tiled=True, axis_index_groups=lines
        )

    def together(*values):
        return lax.optimization_barrier(values)

    def team_sends(value):
        return [value, swap(value, 2), swap(value, 4), swap(value, 6)]

    def team_joins(values):
        near = jnp.stack(values)
        return near, swap(near, 1)

    def team_scatter(keep, *sent):
        own, *sends = halve(keep, [swap(a, 1) for a in sent])
        return own, [swap(s, 2 * j + 2) for j, s in enumerate(sends)]

    small_width = -(-(count + 4) // 128) * 128
    pack_out = shaped(BF16, TEAM, rows, 3 * part + small_width + teams * block)
    pack = pl.pallas_call(
        functools.partial(pack_kernel, teams=teams),
        out_shape=pack_out,
        compiler_params=params(56),
        cost_estimate=cost(),
        name="pack",
    )(
        joint_weight,
        up_weight,
        router_weight,
        mix_weight.T,
        gain_attend[None],
        gain_feed[None],
    )
    pack, merge_weight = together(pack, merge_weight)
    pack = team_exchange(pack).reshape(TEAM * rows, -1)
    placing, g_rows = place_rows(routes, cotangent, count, capacity)
    from_team = lambda d: [
        ((g + d) % teams * TEAM + p, g * TEAM + p) for g in range(teams) for p in range(TEAM)
    ]
    merge_line = [merge_weight]
    merge_line += [lax.ppermute(merge_weight, "expert", from_team(d)) for d in range(1, teams)]
    pack, tokens, g_rows, *merge_line = together(pack, tokens, g_rows, *merge_line)
    joint_rows, g_rows = together(pack[:, : 3 * part + small_width], g_rows)
    g_rows = exchange(g_rows.reshape(count, capacity, width)).reshape(count * capacity, width)
    merge_line = jnp.concatenate(merge_line, axis=0)
    wide = 3 * part + small_width
    x_sent = jnp.concatenate(
        [
            tokens,
            jnp.pad(segments.astype(BF16), ((0, 15), (0, width - length))),
        ],
        axis=0,
    )
    got = line_gather(joint_rows)
    sends = team_sends(x_sent)
    xs = [jnp.stack(sends[:2]), jnp.stack(sends[2:])]
    *xs, pack, g_rows = together(*xs, pack, g_rows)
    xs = xs + [swap(x, 1) for x in xs]
    up_part = line_gather(pack[:, 3 * part + small_width :])
    merge_parts = team_sends(merge_line)

    joint, attended = attend(place_arg, xs, got, length, count)
    attended, *merge_parts = together(attended, *merge_parts)
    merge_near, merge_far = team_joins(merge_parts)
    arrived = team_exchange(attended)
    merge = order(place_arg, merge_near, merge_far, teams).reshape(width, width)
    residual, second, attended, stats, outgoing = middle(
        arrived, merge, tokens, got, routes, placing, count
    )
    received = exchange(outgoing.reshape(count, capacity, -1)).reshape(count * capacity, -1)
    s_near, attended, up_part = together(jnp.stack(team_sends(second)), attended, up_part)
    s_far = swap(s_near, 1)
    a_parts = team_sends(jnp.concatenate([attended, cotangent], axis=0))
    received, s_near, s_far, down_own = together(received, s_near, s_far, down_weight)
    down_part = line_gather(down_own)
    act, d_eupper, back, d_out = expert(received, g_rows, widen_weight, narrow_weight)
    back, s_near, up_part, *a_parts = together(back, s_near, up_part, *a_parts)
    g_near, g_far = team_joins([a[length:] for a in a_parts])
    a_parts = [a[:length] for a in a_parts]
    back = exchange(back.reshape(count, capacity, -1)).reshape(count * capacity, -1)
    keep, low, high, keep_dense, send_dense, up_grad, down_grad = feed(
        s_near, s_far, g_near, g_far, up_part, down_part, got, count
    )
    up_grad = line_scatter(up_grad)
    own, others = team_scatter(keep, low, high)
    own, send_dense, down_grad, d_eupper = together(own, send_dense, down_grad, d_eupper)
    down_grad = line_scatter(down_grad)
    widen_grad = widen_grads(received, d_eupper, width)
    back, widen_grad = together(back, widen_grad)
    a_near, a_far = team_joins(a_parts)
    dense, more = team_scatter(keep_dense, send_dense)
    result, d_residual, side, d_both = after(
        own, others, back, placing, residual, stats, cotangent, got, merge, routes, second, count
    )
    d_both, act = together(d_both, act)
    d_both = team_exchange(d_both)
    narrow_grad = narrow_grads(d_out, act)
    d_both, narrow_grad, up_grad = together(d_both, narrow_grad, up_grad)
    up_grad = team_exchange(up_grad.reshape(TEAM, rows, -1))
    keep, send, grads = attend_back(
        place_arg, xs, a_near, a_far, got, joint, d_both, side, count
    )
    grads, send, up_grad, down_grad = together(grads, send, up_grad, down_grad)
    grads = exchange(grads.reshape(count, rows, -1))
    own, others = team_scatter(keep, send)
    tokens_grad, result = last(
        own, others, dense, more, result, stats, tokens, d_residual, got, count
    )
    grads, tokens_grad = together(grads, tokens_grad)
    grads = grads.reshape(teams, TEAM, rows, -1)
    joint_grad, merge_grad, up_grad, attend_grad, feed_grad, router_grad, mix_grad = owner_sums(
        grads, up_grad, width, hidden, count
    )
    return (
        result,
        tokens_grad,
        attend_grad.reshape(rows),
        joint_grad,
        merge_grad,
        feed_grad.reshape(rows),
        up_grad,
        down_grad.astype(F32),
        router_grad,
        mix_grad.T,
        widen_grad,
        narrow_grad,
    )


def solution(mesh):
    one, two, three = P("expert"), P("expert", None), P("expert", None, None)
    return jax.shard_map(
        body,
        mesh=mesh,
        in_specs=(two, one, two, two, one, two, two, two, two, three, three, two, two, two),
        out_specs=(two, two, one, two, two, one, two, two, two, two, three, three),
        check_vma=False,
    )
```

profile of v0, /device:TPU:0, one launch (start us, length us, event | category | flops | bytes accessed | tf_op | source)
XLA Modules:
  0.0 272.8 jit_solution(14795141404482977349)
XLA Ops:
  7.2 2.0 pack.1
  9.2 5.3 %all-to-all-start = ((bf16[8,32,1024]{2,1,0:T(8,128)(2,1)}), bf16[8,32,1024]{2,1,0:T(8,128)(2,1)S(1)}, u32[]{:S(2)}, u32[]{:S(2)}) async-start(bf16[8,32,1024]{2,1,0:T(8,128)(2,1)} %pack.1), calls=%async_computation | async-start | bytes 1048576 | tf_op jit(solution)/shard_map/all_to_all | solution.py:783
  14.5 1.6 collective-permute-start.2
  16.1 2.6 collective-permute-start.1
  18.7 1.3 collective-permute-start
  20.0 1.4 copy.26.routes_ref
  21.4 2.5 place_rows.1
  25.0 5.2 %all-to-all-start.1 = ((bf16[32,8,1024]{2,1,0:T(8,128)(2,1)}), bf16[32,8,1024]{2,1,0:T(8,128)(2,1)S(1)}, u32[]{:S(2)}, u32[]{:S(2)}) async-start(bf16[32,8,1024]{2,1,0:T(8,128)(2,1)} %bitcast.59), calls=%async_computation.1 | async-start | bytes 1048576 | tf_op jit(solution)/shard_map/all_to_all | solution.py:780
  31.0 1.8 collective-permute-start.3
  32.9 1.5 collective-permute-start.4
  35.2 10.1 %collective-permute-done.3 = bf16[144,1024]{1,0:T(8,128)(2,1)S(1)} collective-permute-done((bf16[144,1024]{1,0:T(8,128)(2,1)S(1)}, bf16[144,1024]{1,0:T(8,128)(2,1)S(1)}, u32[]{:S(2)}, u32[]{:S(2)}) %collective-permute-start.3) | collective-permute-done | bytes 294944 | tf_op jit(solution)/shard_map/ppermute | solution.py:777
  45.6 6.6 %collective-permute-done.5 = bf16[144,1024]{1,0:T(8,128)(2,1)S(1)} collective-permute-done((bf16[144,1024]{1,0:T(8,128)(2,1)S(1)}, bf16[144,1024]{1,0:T(8,128)(2,1)S(1)}, u32[]{:S(2)}, u32[]{:S(2)}) %collective-permute-start.5) | collective-permute-done | bytes 294944 | tf_op jit(solution)/shard_map/ppermute | solution.py:777
  52.8 1.5 constant_dynamic-update-slice_fusion.2
  56.5 1.5 collective-permute-start.9
  58.0 1.1 collective-permute-start.8
  60.4 1.9 all-gather.4.cloned.1.call-done.got_ref.small_ref
  64.0 7.1 %attend.1 = (bf16[8,128,384]{2,1,0:T(8,128)(2,1)}, bf16[8,128,128]{2,1,0:T(8,128)(2,1)}) custom-call(s32[2]{0:T(128)} %pad_add_fusion.place_ref, bf16[2,144,1024]{2,1,0:T(8,128)(2,1)} %copy-done.16, bf16[2,144,1024]{2,1,0:T(8,128)(2,1)} %copy-done.17, bf16[2,144,1024]{2,1,0:T(8,128)(2,1)} %copy-done.24, bf16[2,144,1024]{2,1,0:T(8,128)(2,1)} %copy-done.25, ...), custom_call_target="tpu_custom_call" | custom-call | flops 1 | bytes 1 | tf_op jit(solution)/shard_map/attend/pallas_call | solution.py:159
  71.1 1.4 pad_maximum_fusion.near_ref
  72.6 3.8 %all-to-all-start.2 = ((bf16[8,128,128]{2,1,0:T(8,128)(2,1)}), bf16[8,128,128]{2,1,0:T(8,128)(2,1)S(1)}, u32[]{:S(2)}, u32[]{:S(2)}) async-start(bf16[8,128,128]{2,1,0:T(8,128)(2,1)} %get-tuple-element.126), calls=%async_computation.2 | async-start | bytes 524288 | tf_op jit(solution)/shard_map/all_to_all | solution.py:783
  76.4 1.0 copy-done.22
  77.3 3.0 %order.1 = bf16[4,8,32,1024]{3,2,1,0:T(8,128)(2,1)} custom-call(s32[2]{0:T(128)} %pad_add_fusion.place_ref, bf16[4,128,1024]{2,1,0:T(8,128)(2,1)} %copy-done.15, bf16[4,128,1024]{2,1,0:T(8,128)(2,1)} %copy-done.22), custom_call_target="tpu_custom_call" | custom-call | flops 1 | bytes 1 | tf_op jit(solution)/shard_map/order/pallas_call | solution.py:735
  80.4 2.9 %all-to-all-done.2.att_ref = bf16[8,128,128]{2,1,0:T(8,128)(2,1)S(1)} async-done(((bf16[8,128,128]{2,1,0:T(8,128)(2,1)}), bf16[8,128,128]{2,1,0:T(8,128)(2,1)S(1)}, u32[]{:S(2)}, u32[]{:S(2)}) %all-to-all-start.2) | async-done | bytes 262176 | tf_op jit(solution)/shard_map/all_to_all | solution.py:783
  84.0 4.1 %middle.1 = (f32[128,1024]{1,0:T(8,128)}, bf16[128,1024]{1,0:T(8,128)(2,1)}, bf16[128,1024]{1,0:T(8,128)(2,1)}, f32[128,128]{1,0:T(8,128)}, bf16[256,1152]{1,0:T(8,128)(2,1)}) custom-call(bf16[8,128,128]{2,1,0:T(8,128)(2,1)} %copy-done.23, bf16[1024,1024]{1,0:T(8,128)(2,1)} %bitcast.49, bf16[128,1024]{1,0:T(8,128)(2,1)} %x_ref.1, ...), custom_call_target="tpu_custom_call" | custom-call | flops 1 | bytes 1 | tf_op jit(solution)/shard_map/middle/pallas_call | solution.py:336
  88.7 1.5 collective-permute-start.13
  90.2 1.4 collective-permute-start.12
  91.6 2.6 all-to-all-start.3
  94.3 4.2 %collective-permute-done.14 = bf16[128,1024]{1,0:T(8,128)(2,1)S(1)} collective-permute-done((bf16[128,1024]{1,0:T(8,128)(2,1)}, bf16[128,1024]{1,0:T(8,128)(2,1)S(1)}, u32[]{:S(2)}, u32[]{:S(2)}) %collective-permute-start.14) | collective-permute-done | bytes 262176 | tf_op jit(solution)/shard_map/ppermute | solution.py:777
  98.5 7.6 %collective-permute-done.13 = bf16[128,1024]{1,0:T(8,128)(2,1)S(1)} collective-permute-done((bf16[128,1024]{1,0:T(8,128)(2,1)}, bf16[128,1024]{1,0:T(8,128)(2,1)S(1)}, u32[]{:S(2)}, u32[]{:S(2)}) %collective-permute-start.13) | collective-permute-done | bytes 262176 | tf_op jit(solution)/shard_map/ppermute | solution.py:777
  106.2 1.1 pad_maximum_fusion.1.near_ref
  107.4 1.2 constant_dynamic-update-slice_fusion.5
  108.6 2.3 collective-permute-start.18
  113.0 16.2 %expert.1 = (bf16[256,4096]{1,0:T(8,128)(2,1)}, bf16[256,4096]{1,0:T(8,128)(2,1)}, bf16[256,2048]{1,0:T(8,128)(2,1)}, bf16[256,1024]{1,0:T(8,128)(2,1)}) custom-call(bf16[256,1152]{1,0:T(8,128)(2,1)} %bitcast.51, bf16[256,1024]{1,0:T(8,128)(2,1)} %bitcast.53, bf16[1,1024,4096]{2,1,0:T(8,128)(2,1)} %widen_hbm.1, bf16[1,4096,1024]{2,1,0:T(8,128)(2,1)} %narrow_hbm.1), custom_call_target="tpu_custom_call" | custom-call | flops 1 | bytes 1 | tf_op jit(solution)/shard_map/expert/pallas_call | solution.py:400
  129.3 5.7 %collective-permute-done.17 = bf16[256,1024]{1,0:T(8,128)(2,1)} collective-permute-done((bf16[256,1024]{1,0:T(8,128)(2,1)S(1)}, bf16[256,1024]{1,0:T(8,128)(2,1)}, u32[]{:S(2)}, u32[]{:S(2)}) %collective-permute-start.17) | collective-permute-done | bytes 524320 | tf_op jit(solution)/shard_map/ppermute | solution.py:777
  135.0 1.1 slice_bitcast_fusion.2
  136.1 1.3 slice_bitcast_fusion
  137.6 3.9 %all-to-all-start.4 = ((bf16[32,8,2048]{2,1,0:T(8,128)(2,1)}), bf16[32,8,2048]{2,1,0:T(8,128)(2,1)}, u32[]{:S(2)}, u32[]{:S(2)}) async-start(bf16[32,8,2048]{2,1,0:T(8,128)(2,1)} %bitcast.31), calls=%async_computation.4 | async-start | bytes 2097152 | tf_op jit(solution)/shard_map/all_to_all | solution.py:780
  142.8 12.4 %feed.1 = (f32[4,128,1152]{2,1,0:T(8,128)}, bf16[4,128,512]{2,1,0:T(8,128)(2,1)}, bf16[4,128,640]{2,1,0:T(8,128)(2,1)}, f32[4,128,1024]{2,1,0:T(8,128)}, bf16[4,...) custom-call(bf16[4,128,1024]{2,1,0:T(8,128)(2,1)} %copy-done.13, ...), custom_call_target="tpu_custom_call" | custom-call | flops 1 | bytes 1 | tf_op jit(solution)/shard_map/feed/pallas_call | solution.py:520
  155.7 1.1 pad_maximum_fusion.2.near_att
  157.0 1.3 collective-permute-done.21.refs_0_
  159.4 1.7 collective-permute-start.23
  161.1 1.5 collective-permute-start.24
  162.8 9.7 %widen_grads.1 = f32[1,1024,4096]{2,1,0:T(8,128)} custom-call(bf16[256,1152]{1,0:T(8,128)(2,1)} %bitcast.52, bf16[256,4096]{1,0:T(8,128)(2,1)} %get-tuple-element.164.d_ref), custom_call_target="tpu_custom_call" | custom-call | flops 1 | bytes 1 | tf_op jit(solution)/shard_map/widen_grads/pallas_call | solution.py:453
  172.5 2.0 all-to-all-done.4
  174.6 1.6 collective-permute-done.24.r2_ref
  176.2 1.4 collective-permute-done.25.r3_ref
  178.4 5.7 %after.1 = (f32[128,1024]{1,0:T(8,128)}, f32[128,1024]{1,0:T(8,128)}, f32[1024,128]{1,0:T(8,128)}, bf16[8,256,128]{2,1,0:T(8,128)(2,1)}) custom-call(f32[128,1152]{1,0:T(8,128)} %copy-done.8, bf16[128,1152]{1,0:T(8,128)(2,1)} %copy-done.27, bf16[128,1152]{1,0:T(8,128)(2,1)} %copy-done.28, bf16[128,1152]{1,0:T(8,128)(2,1)} %copy-done.29, ...), custom_call_target="tpu_custom_call" | custom-call | flops 1 | bytes 1 | tf_op jit(solution)/shard_map/after/pallas_call | solution.py:616
  184.0 3.5 %all-to-all-start.5 = ((bf16[8,256,128]{2,1,0:T(8,128)(2,1)}), bf16[8,256,128]{2,1,0:T(8,128)(2,1)S(1)}, u32[]{:S(2)}, u32[]{:S(2)}) async-start(bf16[8,256,128]{2,1,0:T(8,128)(2,1)} %get-tuple-element.170), calls=%async_computation.5 | async-start | bytes 1048576 | tf_op jit(solution)/shard_map/all_to_all | solution.py:783
  188.1 9.5 %narrow_grads.1 = f32[1,4096,1024]{2,1,0:T(8,128)} custom-call(bf16[256,1024]{1,0:T(8,128)(2,1)} %get-tuple-element.171.rows_ref, bf16[256,4096]{1,0:T(8,128)(2,1)} %get-tuple-element.172.act_ref), custom_call_target="tpu_custom_call" | custom-call | flops 1 | bytes 1 | tf_op jit(solution)/shard_map/narrow_grads/pallas_call | solution.py:431
  197.6 4.1 %all-to-all-start.6 = ((bf16[8,32,512]{2,1,0:T(8,128)(2,1)}), bf16[8,32,512]{2,1,0:T(8,128)(2,1)S(1)}, u32[]{:S(2)}, u32[]{:S(2)}) async-start(bf16[8,32,512]{2,1,0:T(8,128)(2,1)} %bitcast.64), calls=%async_computation.7 | async-start | bytes 524288 | tf_op jit(solution)/shard_map/all_to_all | solution.py:783
  201.8 13.2 %attend_back.1 = (f32[4,128,1024]{2,1,0:T(8,128)}, bf16[4,128,1024]{2,1,0:T(8,128)(2,1)}, bf16[1024,640]{1,0:T(8,128)(2,1)}) custom-call(s32[2]{0:T(128)} %pad_add_fusion.place_ref, bf16[2,144,1024]{2,1,0:T(8,128)(2,1)} %copy-done.16, bf16[2,144,1024]{2,1,0:T(8,128)(2,1)} %copy-done.17, bf16[2,144,1024]{2,1,0:T(8,128)(2,1)} %copy-done.24, ...), custom_call_target="tpu_custom_call" | custom-call | flops 20000000000 | bytes 1 | tf_op jit(solution)/shard_map/attend_back/pallas_call | solution.py:242
  215.7 3.0 %reduce-scatter.5.cloned.1.call-done = bf16[128,1024]{1,0:T(8,128)(2,1)} async-done(((bf16[512,1024]{1,0:T(8,128)(2,1)}), bf16[128,1024]{1,0:T(8,128)(2,1)}) %reduce-scatter.5.cloned.1.call-update) | async-done | bytes 262160 | tf_op jit(solution)/shard_map/reduce_scatter | solution.py:789
  218.7 3.3 %all-to-all-start.7 = ((bf16[32,32,640]{2,1,0:T(8,128)(2,1)}), bf16[32,32,640]{2,1,0:T(8,128)(2,1)S(1)}, u32[]{:S(2)}, u32[]{:S(2)}) async-start(bf16[32,32,640]{2,1,0:T(8,128)(2,1)} %bitcast.56), calls=%async_computation.9 | async-start | bytes 2621440 | tf_op jit(solution)/shard_map/all_to_all | solution.py:780
  222.6 2.4 collective-permute-done.30.refs_0_
  225.2 1.8 collective-permute-start.31
  227.0 1.5 collective-permute-start.32
  229.0 1.8 collective-permute-start.27
  230.8 1.5 collective-permute-start.28
  232.3 10.8 %collective-permute-done.31.d1_ref = bf16[128,1024]{1,0:T(8,128)(2,1)S(1)} collective-permute-done((bf16[128,1024]{1,0:T(8,128)(2,1)S(1)}, bf16[128,1024]{1,0:T(8,128)(2,1)S(1)}, u32[]{:S(2)}, u32[]{:S(2)}) %collective-permute-start.31) | collective-permute-done | bytes 262176 | tf_op jit(solution)/shard_map/ppermute | solution.py:777
  243.1 1.6 collective-permute-start.29
  245.5 6.0 %collective-permute-done.33.d3_ref = bf16[128,1024]{1,0:T(8,128)(2,1)S(1)} collective-permute-done((bf16[128,1024]{1,0:T(8,128)(2,1)S(1)}, bf16[128,1024]{1,0:T(8,128)(2,1)S(1)}, u32[]{:S(2)}, u32[]{:S(2)}) %collective-permute-start.33) | collective-permute-done | bytes 262176 | tf_op jit(solution)/shard_map/ppermute | solution.py:777
  251.5 5.5 %collective-permute-done.27.r1_ref = bf16[128,1024]{1,0:T(8,128)(2,1)S(1)} collective-permute-done((bf16[128,1024]{1,0:T(8,128)(2,1)S(1)}, bf16[128,1024]{1,0:T(8,128)(2,1)S(1)}, u32[]{:S(2)}, u32[]{:S(2)}) %collective-permute-start.27) | collective-permute-done | bytes 262176 | tf_op jit(solution)/shard_map/ppermute | solution.py:777
  257.1 5.8 %collective-permute-done.29.r3_ref = bf16[128,1024]{1,0:T(8,128)(2,1)S(1)} collective-permute-done((bf16[128,1024]{1,0:T(8,128)(2,1)S(1)}, bf16[128,1024]{1,0:T(8,128)(2,1)S(1)}, u32[]{:S(2)}, u32[]{:S(2)}) %collective-permute-start.29) | collective-permute-done | bytes 262176 | tf_op jit(solution)/shard_map/ppermute | solution.py:777
  262.9 2.2 last.1
  265.1 1.2 owner_sums.1
  (140 shorter events, 20.3 us)
Async XLA Ops:
  7.2 23.8 %copy-start.33 = (s32[1,128]{1,0:T(1,128)S(1)}, s32[1,128]{1,0:T(1,128)}, u32[]{:S(2)}) copy-start(s32[1,128]{1,0:T(1,128)} %param.26) | copy-start | bytes 1540
  7.2 23.8 %copy-start.2 = (bf16[128,1024]{1,0:T(8,128)(2,1)S(1)}, bf16[128,1024]{1,0:T(8,128)(2,1)}, u32[]{:S(2)}) copy-start(bf16[128,1024]{1,0:T(8,128)(2,1)} %x_ref.1) | copy-start | bytes 786436
  9.2 25.4 %copy-start.31 = (bf16[32,1024]{1,0:T(8,128)(2,1)S(1)}, bf16[32,1024]{1,0:T(8,128)(2,1)}, u32[]{:S(2)}) copy-start(bf16[32,1024]{1,0:T(8,128)(2,1)} %param.17) | copy-start | bytes 196612
  9.2 15.0 %all-to-all-start = ((bf16[8,32,1024]{2,1,0:T(8,128)(2,1)}), bf16[8,32,1024]{2,1,0:T(8,128)(2,1)S(1)}, u32[]{:S(2)}, u32[]{:S(2)}) async-start(bf16[8,32,1024]{2,1,0:T(8,128)(2,1)} %pack.1), calls=%async_computation | async-start | bytes 1048576 | tf_op jit(solution)/shard_map/all_to_all | solution.py:783
  14.5 9.4 %collective-permute-start.2 = (bf16[32,1024]{1,0:T(8,128)(2,1)}, bf16[32,1024]{1,0:T(8,128)(2,1)S(1)}, u32[]{:S(2)}, u32[]{:S(2)}) collective-permute-start(bf16[32,1024]{1,0:T(8,128)(2,1)} %param.17), channel_id=1, source_target_pairs={{24,0},{25,1},{26,2},{27,3},{28,4},{29,5},{30,6},{31,7},{0,8},{1,9... | collective-permute-start | bytes 196616 | tf_op jit(solution)/shard_map/ppermute | solution.py:830
  16.1 7.9 %collective-permute-start.1 = (bf16[32,1024]{1,0:T(8,128)(2,1)}, bf16[32,1024]{1,0:T(8,128)(2,1)S(1)}, u32[]{:S(2)}, u32[]{:S(2)}) collective-permute-start(bf16[32,1024]{1,0:T(8,128)(2,1)} %param.17), channel_id=1, source_target_pairs={{16,0},{17,1},{18,2},{19,3},{20,4},{21,5},{22,6},{23,7},{24,8},{25... | collective-permute-start | bytes 196616 | tf_op jit(solution)/shard_map/ppermute | solution.py:830
  18.7 5.6 %collective-permute-start = (bf16[32,1024]{1,0:T(8,128)(2,1)}, bf16[32,1024]{1,0:T(8,128)(2,1)S(1)}, u32[]{:S(2)}, u32[]{:S(2)}) collective-permute-start(bf16[32,1024]{1,0:T(8,128)(2,1)} %param.17), channel_id=1, source_target_pairs={{8,0},{9,1},{10,2},{11,3},{12,4},{13,5},{14,6},{15,7},{16,8},{17,9... | collective-permute-start | bytes 196616 | tf_op jit(solution)/shard_map/ppermute | solution.py:830
  25.0 27.3 %all-to-all-start.1 = ((bf16[32,8,1024]{2,1,0:T(8,128)(2,1)}), bf16[32,8,1024]{2,1,0:T(8,128)(2,1)S(1)}, u32[]{:S(2)}, u32[]{:S(2)}) async-start(bf16[32,8,1024]{2,1,0:T(8,128)(2,1)} %bitcast.59), calls=%async_computation.1 | async-start | bytes 1048576 | tf_op jit(solution)/shard_map/all_to_all | solution.py:780
  30.2 32.2 %all-gather.4.cloned.1.call-start = ((), (), s32[]{:S(2)}) async-start(), calls=%async_computation.10 | async-start | bytes 1310720 | tf_op jit(solution)/shard_map/all_gather | solution.py:786
  30.9 76.4 %all-gather.6.cloned.1.call-start = ((), (), s32[]{:S(2)}) async-start(), calls=%async_computation.11 | async-start | bytes 1310720 | tf_op jit(solution)/shard_map/all_gather | solution.py:786
  31.0 14.3 %collective-permute-start.3 = (bf16[144,1024]{1,0:T(8,128)(2,1)S(1)}, bf16[144,1024]{1,0:T(8,128)(2,1)S(1)}, u32[]{:S(2)}, u32[]{:S(2)}) collective-permute-start(bf16[144,1024]{1,0:T(8,128)(2,1)S(1)} %get-tuple-element.219), channel_id=1, source_target_pairs={{0,2},{1,3},{2,0},{3,1},{4,6},{5,7},{6,4},{7,5},{8,10},{9,11},{10,... | collective-permute-start | bytes 884744 | tf_op jit(solution)/shard_map/ppermute | solution.py:777
  32.9 12.7 %collective-permute-start.4 = (bf16[144,1024]{1,0:T(8,128)(2,1)S(1)}, bf16[144,1024]{1,0:T(8,128)(2,1)S(1)}, u32[]{:S(2)}, u32[]{:S(2)}) collective-permute-start(bf16[144,1024]{1,0:T(8,128)(2,1)S(1)} %get-tuple-element.219), channel_id=1, source_target_pairs={{0,4},{1,5},{2,6},{3,7},{4,0},{5,1},{6,2},{7,3},{8,12},{9,13},{10,... | collective-permute-start | bytes 884744 | tf_op jit(solution)/shard_map/ppermute | solution.py:777
  34.3 17.8 %collective-permute-start.5 = (bf16[144,1024]{1,0:T(8,128)(2,1)S(1)}, bf16[144,1024]{1,0:T(8,128)(2,1)S(1)}, u32[]{:S(2)}, u32[]{:S(2)}) collective-permute-start(bf16[144,1024]{1,0:T(8,128)(2,1)S(1)} %get-tuple-element.219), channel_id=1, source_target_pairs={{0,6},{1,7},{2,4},{3,5},{4,2},{5,3},{6,0},{7,1},{8,14},{9,15},{10,... | collective-permute-start | bytes 884744 | tf_op jit(solution)/shard_map/ppermute | solution.py:777
  45.4 16.9 %copy-start.16 = (bf16[2,144,1024]{2,1,0:T(8,128)(2,1)}, bf16[2,144,1024]{2,1,0:T(8,128)(2,1)S(1)}, u32[]{:S(2)}) copy-start(bf16[2,144,1024]{2,1,0:T(8,128)(2,1)S(1)} %pad_maximum_fusion.4.n0_ref) | copy-start | bytes 1769476
  52.2 10.1 %copy-start.17 = (bf16[2,144,1024]{2,1,0:T(8,128)(2,1)}, bf16[2,144,1024]{2,1,0:T(8,128)(2,1)S(1)}, u32[]{:S(2)}) copy-start(bf16[2,144,1024]{2,1,0:T(8,128)(2,1)S(1)} %pad_maximum_fusion.5.n1_ref) | copy-start | bytes 1769476
  52.3 18.9 %copy-start.19 = (bf16[32,8,1024]{2,1,0:T(8,128)(2,1)}, bf16[32,8,1024]{2,1,0:T(8,128)(2,1)S(1)}, u32[]{:S(2)}) copy-start(bf16[32,8,1024]{2,1,0:T(8,128)(2,1)S(1)} %all-to-all-done.1) | copy-start | bytes 1572868
  52.3 10.1 %collective-permute-start.6 = (bf16[2,144,1024]{2,1,0:T(8,128)(2,1)S(1)}, bf16[2,144,1024]{2,1,0:T(8,128)(2,1)S(1)}, u32[]{:S(2)}, u32[]{:S(2)}) collective-permute-start(bf16[2,144,1024]{2,1,0:T(8,128)(2,1)S(1)} %pad_maximum_fusion.4.n0_ref), channel_id=1, source_target_pairs={{0,1},{1,0},{2,3},{3,2},{4,5},{5,4},{6,7},{7,6},{8,9},{9,8},{10,11... | collective-permute-start | bytes 1769480 | tf_op jit(solution)/shard_map/ppermute | solution.py:777
  52.4 10.0 %collective-permute-start.7 = (bf16[2,144,1024]{2,1,0:T(8,128)(2,1)S(1)}, bf16[2,144,1024]{2,1,0:T(8,128)(2,1)S(1)}, u32[]{:S(2)}, u32[]{:S(2)}) collective-permute-start(bf16[2,144,1024]{2,1,0:T(8,128)(2,1)S(1)} %pad_maximum_fusion.5.n1_ref), channel_id=1, source_target_pairs={{0,1},{1,0},{2,3},{3,2},{4,5},{5,4},{6,7},{7,6},{8,9},{9,8},{10,11... | collective-permute-start | bytes 1769480 | tf_op jit(solution)/shard_map/ppermute | solution.py:777
  55.6 15.5 %collective-permute-start.10 = (bf16[128,1024]{1,0:T(8,128)(2,1)}, bf16[128,1024]{1,0:T(8,128)(2,1)}, u32[]{:S(2)}, u32[]{:S(2)}) collective-permute-start(bf16[128,1024]{1,0:T(8,128)(2,1)} %constant_dynamic-update-slice_fusion), channel_id=1, source_target_pairs={{0,6},{1,7},{2,4},{3,5},{4,2},{5,3},{6,0},{7,1},{8,14},{9,15},{10,... | collective-permute-start | bytes 786440 | tf_op jit(solution)/shard_map/ppermute | solution.py:777
  56.5 14.6 %collective-permute-start.9 = (bf16[128,1024]{1,0:T(8,128)(2,1)}, bf16[128,1024]{1,0:T(8,128)(2,1)}, u32[]{:S(2)}, u32[]{:S(2)}) collective-permute-start(bf16[128,1024]{1,0:T(8,128)(2,1)} %constant_dynamic-update-slice_fusion), channel_id=1, source_target_pairs={{0,4},{1,5},{2,6},{3,7},{4,0},{5,1},{6,2},{7,3},{8,12},{9,13},{10,... | collective-permute-start | bytes 786440 | tf_op jit(solution)/shard_map/ppermute | solution.py:777
  58.0 13.2 %collective-permute-start.8 = (bf16[128,1024]{1,0:T(8,128)(2,1)}, bf16[128,1024]{1,0:T(8,128)(2,1)}, u32[]{:S(2)}, u32[]{:S(2)}) collective-permute-start(bf16[128,1024]{1,0:T(8,128)(2,1)} %constant_dynamic-update-slice_fusion), channel_id=1, source_target_pairs={{0,2},{1,3},{2,0},{3,1},{4,6},{5,7},{6,4},{7,5},{8,10},{9,11},{10,... | collective-permute-start | bytes 786440 | tf_op jit(solution)/shard_map/ppermute | solution.py:777
  72.5 3.8 %collective-permute-start.11 = (bf16[4,128,1024]{2,1,0:T(8,128)(2,1)S(1)}, bf16[4,128,1024]{2,1,0:T(8,128)(2,1)S(1)}, u32[]{:S(2)}, u32[]{:S(2)}) collective-permute-start(bf16[4,128,1024]{2,1,0:T(8,128)(2,1)S(1)} %pad_maximum_fusion.near_ref), channel_id=1, source_target_pairs={{0,1},{1,0},{2,3},{3,2},{4,5},{5,4},{6,7},{7,6},{8,9},{9,8},{10,11... | collective-permute-start | bytes 3145736 | tf_op jit(solution)/shard_map/ppermute | solution.py:777
  72.6 10.7 %all-to-all-start.2 = ((bf16[8,128,128]{2,1,0:T(8,128)(2,1)}), bf16[8,128,128]{2,1,0:T(8,128)(2,1)S(1)}, u32[]{:S(2)}, u32[]{:S(2)}) async-start(bf16[8,128,128]{2,1,0:T(8,128)(2,1)} %get-tuple-element.126), calls=%async_computation.2 | async-start | bytes 524288 | tf_op jit(solution)/shard_map/all_to_all | solution.py:783
  88.1 20.4 %copy-start.18 = (bf16[128,1024]{1,0:T(8,128)(2,1)S(1)}, bf16[128,1024]{1,0:T(8,128)(2,1)}, u32[]{:S(2)}) copy-start(bf16[128,1024]{1,0:T(8,128)(2,1)} %g_ref.3) | copy-start | bytes 786436
  88.1 10.4 %collective-permute-start.14 = (bf16[128,1024]{1,0:T(8,128)(2,1)}, bf16[128,1024]{1,0:T(8,128)(2,1)S(1)}, u32[]{:S(2)}, u32[]{:S(2)}) collective-permute-start(bf16[128,1024]{1,0:T(8,128)(2,1)} %get-tuple-element.133.second_ref), channel_id=1, source_target_pairs={{0,6},{1,7},{2,4},{3,5},{4,2},{5,3},{6,0},{7,1},{8,14},{9,15},{10,... | collective-permute-start | bytes 786440 | tf_op jit(solution)/shard_map/ppermute | solution.py:777
  88.7 17.5 %collective-permute-start.13 = (bf16[128,1024]{1,0:T(8,128)(2,1)}, bf16[128,1024]{1,0:T(8,128)(2,1)S(1)}, u32[]{:S(2)}, u32[]{:S(2)}) collective-permute-start(bf16[128,1024]{1,0:T(8,128)(2,1)} %get-tuple-element.133.second_ref), channel_id=1, source_target_pairs={{0,4},{1,5},{2,6},{3,7},{4,0},{5,1},{6,2},{7,3},{8,12},{9,13},{10,... | collective-permute-start | bytes 786440 | tf_op jit(solution)/shard_map/ppermute | solution.py:777
  90.2 16.0 %collective-permute-start.12 = (bf16[128,1024]{1,0:T(8,128)(2,1)}, bf16[128,1024]{1,0:T(8,128)(2,1)S(1)}, u32[]{:S(2)}, u32[]{:S(2)}) collective-permute-start(bf16[128,1024]{1,0:T(8,128)(2,1)} %get-tuple-element.133.second_ref), channel_id=1, source_target_pairs={{0,2},{1,3},{2,0},{3,1},{4,6},{5,7},{6,4},{7,5},{8,10},{9,11},{10,... | collective-permute-start | bytes 786440 | tf_op jit(solution)/shard_map/ppermute | solution.py:777
  91.6 20.5 %all-to-all-start.3 = ((bf16[32,8,1152]{2,1,0:T(8,128)(2,1)}), bf16[32,8,1152]{2,1,0:T(8,128)(2,1)S(1)}, u32[]{:S(2)}, u32[]{:S(2)}) async-start(bf16[32,8,1152]{2,1,0:T(8,128)(2,1)} %bitcast.58), calls=%async_computation.3 | async-start | bytes 1179648 | tf_op jit(solution)/shard_map/all_to_all | solution.py:780
  94.2 47.6 %all-gather.8.cloned.1.call-start = ((), (), s32[]{:S(2)}) async-start(), calls=%async_computation.12 | async-start | bytes 1310720 | tf_op jit(solution)/shard_map/all_gather | solution.py:786
  107.2 22.0 %copy-start.13 = (bf16[4,128,1024]{2,1,0:T(8,128)(2,1)}, bf16[4,128,1024]{2,1,0:T(8,128)(2,1)S(1)}, u32[]{:S(2)}) copy-start(bf16[4,128,1024]{2,1,0:T(8,128)(2,1)S(1)} %pad_maximum_fusion.1.near_ref) | copy-start | bytes 3145732
  107.3 4.9 %collective-permute-start.15 = (bf16[4,128,1024]{2,1,0:T(8,128)(2,1)S(1)}, bf16[4,128,1024]{2,1,0:T(8,128)(2,1)S(1)}, u32[]{:S(2)}, u32[]{:S(2)}) collective-permute-start(bf16[4,128,1024]{2,1,0:T(8,128)(2,1)S(1)} %pad_maximum_fusion.1.near_ref), channel_id=1, source_target_pairs={{0,1},{1,0},{2,3},{3,2},{4,5},{5,4},{6,7},{7,6},{8,9},{9,8},{10,11... | collective-permute-start | bytes 3145736 | tf_op jit(solution)/shard_map/ppermute | solution.py:777
  108.6 20.7 %collective-permute-start.18 = (bf16[256,1024]{1,0:T(8,128)(2,1)S(1)}, bf16[256,1024]{1,0:T(8,128)(2,1)}, u32[]{:S(2)}, u32[]{:S(2)}) collective-permute-start(bf16[256,1024]{1,0:T(8,128)(2,1)S(1)} %constant_dynamic-update-slice_fusion.4), channel_id=1, source_target_pairs={{0,6},{1,7},{2,4},{3,5},{4,2},{5,3},{6,0},{7,1},{8,14},{9,15},{10,... | collective-permute-start | bytes 1572872 | tf_op jit(solution)/shard_map/ppermute | solution.py:777
  110.9 24.1 %collective-permute-start.17 = (bf16[256,1024]{1,0:T(8,128)(2,1)S(1)}, bf16[256,1024]{1,0:T(8,128)(2,1)}, u32[]{:S(2)}, u32[]{:S(2)}) collective-permute-start(bf16[256,1024]{1,0:T(8,128)(2,1)S(1)} %constant_dynamic-update-slice_fusion.4), channel_id=1, source_target_pairs={{0,4},{1,5},{2,6},{3,7},{4,0},{5,1},{6,2},{7,3},{8,12},{9,13},{10,... | collective-permute-start | bytes 1572872 | tf_op jit(solution)/shard_map/ppermute | solution.py:777
  111.6 23.4 %collective-permute-start.16 = (bf16[256,1024]{1,0:T(8,128)(2,1)S(1)}, bf16[256,1024]{1,0:T(8,128)(2,1)}, u32[]{:S(2)}, u32[]{:S(2)}) collective-permute-start(bf16[256,1024]{1,0:T(8,128)(2,1)S(1)} %constant_dynamic-update-slice_fusion.4), channel_id=1, source_target_pairs={{0,2},{1,3},{2,0},{3,1},{4,6},{5,7},{6,4},{7,5},{8,10},{9,11},{10,... | collective-permute-start | bytes 1572872 | tf_op jit(solution)/shard_map/ppermute | solution.py:777
  112.1 17.1 %copy-start.20 = (bf16[4,128,1024]{2,1,0:T(8,128)(2,1)}, bf16[4,128,1024]{2,1,0:T(8,128)(2,1)S(1)}, u32[]{:S(2)}) copy-start(bf16[4,128,1024]{2,1,0:T(8,128)(2,1)S(1)} %collective-permute-done.15.far_ref) | copy-start | bytes 3145732
  137.6 4.2 %collective-permute-start.20 = (bf16[4,128,1024]{2,1,0:T(8,128)(2,1)S(1)}, bf16[4,128,1024]{2,1,0:T(8,128)(2,1)S(1)}, u32[]{:S(2)}, u32[]{:S(2)}) collective-permute-start(bf16[4,128,1024]{2,1,0:T(8,128)(2,1)S(1)} %pad_maximum_fusion.3.g_near_ref), channel_id=1, source_target_pairs={{0,1},{1,0},{2,3},{3,2},{4,5},{5,4},{6,7},{7,6},{8,9},{9,8},{10,11... | collective-permute-start | bytes 3145736 | tf_op jit(solution)/shard_map/ppermute | solution.py:777
  137.6 37.0 %all-to-all-start.4 = ((bf16[32,8,2048]{2,1,0:T(8,128)(2,1)}), bf16[32,8,2048]{2,1,0:T(8,128)(2,1)}, u32[]{:S(2)}, u32[]{:S(2)}) async-start(bf16[32,8,2048]{2,1,0:T(8,128)(2,1)} %bitcast.31), calls=%async_computation.4 | async-start | bytes 2097152 | tf_op jit(solution)/shard_map/all_to_all | solution.py:780
  141.5 56.1 %reduce-scatter.3.cloned.1.call-start = ((), (), s32[]{:S(2)}) async-start(), calls=%async_computation.13 | async-start | bytes 1310720 | tf_op jit(solution)/shard_map/reduce_scatter | solution.py:789
  155.1 3.1 %collective-permute-start.22 = (bf16[4,128,640]{2,1,0:T(8,128)(2,1)}, bf16[4,128,640]{2,1,0:T(8,128)(2,1)S(1)}, u32[]{:S(2)}, u32[]{:S(2)}) collective-permute-start(bf16[4,128,640]{2,1,0:T(8,128)(2,1)} %get-tuple-element.154), channel_id=1, source_target_pairs={{0,1},{1,0},{2,3},{3,2},{4,5},{5,4},{6,7},{7,6},{8,9},{9,8},{10,11... | collective-permute-start | bytes 1966088 | tf_op jit(solution)/shard_map/ppermute | solution.py:777
  155.4 2.9 %collective-permute-start.21 = (bf16[4,128,512]{2,1,0:T(8,128)(2,1)}, bf16[4,128,512]{2,1,0:T(8,128)(2,1)S(1)}, u32[]{:S(2)}, u32[]{:S(2)}) collective-permute-start(bf16[4,128,512]{2,1,0:T(8,128)(2,1)} %get-tuple-element.153), channel_id=1, source_target_pairs={{0,1},{1,0},{2,3},{3,2},{4,5},{5,4},{6,7},{7,6},{8,9},{9,8},{10,11... | collective-permute-start | bytes 1572872 | tf_op jit(solution)/shard_map/ppermute | solution.py:777
  156.8 45.0 %collective-permute-start.19 = (bf16[4,128,1024]{2,1,0:T(8,128)(2,1)}, bf16[4,128,1024]{2,1,0:T(8,128)(2,1)}, u32[]{:S(2)}, u32[]{:S(2)}) collective-permute-start(bf16[4,128,1024]{2,1,0:T(8,128)(2,1)} %pad_maximum_fusion.2.near_att), channel_id=1, source_target_pairs={{0,1},{1,0},{2,3},{3,2},{4,5},{5,4},{6,7},{7,6},{8,9},{9,8},{10,11... | collective-permute-start | bytes 3145736 | tf_op jit(solution)/shard_map/ppermute | solution.py:777
  159.4 15.2 %collective-permute-start.23 = (bf16[128,1152]{1,0:T(8,128)(2,1)S(1)}, bf16[128,1152]{1,0:T(8,128)(2,1)S(1)}, u32[]{:S(2)}, u32[]{:S(2)}) collective-permute-start(bf16[128,1152]{1,0:T(8,128)(2,1)S(1)} %get-tuple-element.160), channel_id=1, source_target_pairs={{0,2},{1,3},{2,0},{3,1},{4,6},{5,7},{6,4},{7,5},{8,10},{9,11},{10,... | collective-permute-start | bytes 884744 | tf_op jit(solution)/shard_map/ppermute | solution.py:777
  161.1 15.1 %collective-permute-start.24 = (bf16[128,1152]{1,0:T(8,128)(2,1)S(1)}, bf16[128,1152]{1,0:T(8,128)(2,1)S(1)}, u32[]{:S(2)}, u32[]{:S(2)}) collective-permute-start(bf16[128,1152]{1,0:T(8,128)(2,1)S(1)} %get-tuple-element.161), channel_id=1, source_target_pairs={{0,4},{1,5},{2,6},{3,7},{4,0},{5,1},{6,2},{7,3},{8,12},{9,13},{10,... | collective-permute-start | bytes 884744 | tf_op jit(solution)/shard_map/ppermute | solution.py:777
  162.5 15.1 %collective-permute-start.25 = (bf16[128,1152]{1,0:T(8,128)(2,1)S(1)}, bf16[128,1152]{1,0:T(8,128)(2,1)S(1)}, u32[]{:S(2)}, u32[]{:S(2)}) collective-permute-start(bf16[128,1152]{1,0:T(8,128)(2,1)S(1)} %get-tuple-element.162), channel_id=1, source_target_pairs={{0,6},{1,7},{2,4},{3,5},{4,2},{5,3},{6,0},{7,1},{8,14},{9,15},{10,... | collective-permute-start | bytes 884744 | tf_op jit(solution)/shard_map/ppermute | solution.py:777
  184.0 13.6 %all-to-all-start.5 = ((bf16[8,256,128]{2,1,0:T(8,128)(2,1)}), bf16[8,256,128]{2,1,0:T(8,128)(2,1)S(1)}, u32[]{:S(2)}, u32[]{:S(2)}) async-start(bf16[8,256,128]{2,1,0:T(8,128)(2,1)} %get-tuple-element.170), calls=%async_computation.5 | async-start | bytes 1048576 | tf_op jit(solution)/shard_map/all_to_all | solution.py:783
  187.5 31.2 %reduce-scatter.5.cloned.1.call-start = ((), (), s32[]{:S(2)}) async-start(), calls=%async_computation.14 | async-start | bytes 1310720 | tf_op jit(solution)/shard_map/reduce_scatter | solution.py:789
  197.6 17.3 %all-to-all-start.6 = ((bf16[8,32,512]{2,1,0:T(8,128)(2,1)}), bf16[8,32,512]{2,1,0:T(8,128)(2,1)S(1)}, u32[]{:S(2)}, u32[]{:S(2)}) async-start(bf16[8,32,512]{2,1,0:T(8,128)(2,1)} %bitcast.64), calls=%async_computation.7 | async-start | bytes 524288 | tf_op jit(solution)/shard_map/all_to_all | solution.py:783
  215.0 9.9 %copy-start.4 = (f32[4,128,1024]{2,1,0:T(8,128)S(1)}, f32[4,128,1024]{2,1,0:T(8,128)}, u32[]{:S(2)}) copy-start(f32[4,128,1024]{2,1,0:T(8,128)} %get-tuple-element.186.keep_ref) | copy-start | bytes 6291460
  218.7 46.4 %all-to-all-start.7 = ((bf16[32,32,640]{2,1,0:T(8,128)(2,1)}), bf16[32,32,640]{2,1,0:T(8,128)(2,1)S(1)}, u32[]{:S(2)}, u32[]{:S(2)}) async-start(bf16[32,32,640]{2,1,0:T(8,128)(2,1)} %bitcast.56), calls=%async_computation.9 | async-start | bytes 2621440 | tf_op jit(solution)/shard_map/all_to_all | solution.py:780
  222.0 6.8 %copy-start.5 = (f32[4,128,1024]{2,1,0:T(8,128)S(1)}, f32[4,128,1024]{2,1,0:T(8,128)}, u32[]{:S(2)}) copy-start(f32[4,128,1024]{2,1,0:T(8,128)} %get-tuple-element.176.keep_ref) | copy-start | bytes 6291460
  222.0 2.9 %collective-permute-start.30 = (bf16[4,128,1024]{2,1,0:T(8,128)(2,1)}, bf16[4,128,1024]{2,1,0:T(8,128)(2,1)S(1)}, u32[]{:S(2)}, u32[]{:S(2)}) collective-permute-start(bf16[4,128,1024]{2,1,0:T(8,128)(2,1)} %get-tuple-element.187), channel_id=1, source_target_pairs={{0,1},{1,0},{2,3},{3,2},{4,5},{5,4},{6,7},{7,6},{8,9},{9,8},{10,11... | collective-permute-start | bytes 3145736 | tf_op jit(solution)/shard_map/ppermute | solution.py:777
  222.3 6.5 %collective-permute-start.26 = (bf16[4,128,1024]{2,1,0:T(8,128)(2,1)}, bf16[4,128,1024]{2,1,0:T(8,128)(2,1)S(1)}, u32[]{:S(2)}, u32[]{:S(2)}) collective-permute-start(bf16[4,128,1024]{2,1,0:T(8,128)(2,1)} %get-tuple-element.181), channel_id=1, source_target_pairs={{0,1},{1,0},{2,3},{3,2},{4,5},{5,4},{6,7},{7,6},{8,9},{9,8},{10,11... | collective-permute-start | bytes 3145736 | tf_op jit(solution)/shard_map/ppermute | solution.py:777
  225.1 19.5 %copy-start.30 = (bf16[128,1024]{1,0:T(8,128)(2,1)S(1)}, bf16[128,1024]{1,0:T(8,128)(2,1)}, u32[]{:S(2)}) copy-start(bf16[128,1024]{1,0:T(8,128)(2,1)} %reduce-scatter.5.cloned.1.call-done) | copy-start | bytes 786436
  225.2 37.7 %copy-start = (bf16[1024,512]{1,0:T(8,128)(2,1)S(1)}, bf16[1024,512]{1,0:T(8,128)(2,1)}, u32[]{:S(2)}) copy-start(bf16[1024,512]{1,0:T(8,128)(2,1)} %all-gather.4.cloned.1.call-done.got_ref.small_ref) | copy-start | bytes 3145732
  225.2 37.7 %copy-start.3 = (bf16[128,1024]{1,0:T(8,128)(2,1)S(1)}, bf16[128,1024]{1,0:T(8,128)(2,1)}, u32[]{:S(2)}) copy-start(bf16[128,1024]{1,0:T(8,128)(2,1)} %x_ref.1) | copy-start | bytes 786436
  225.2 37.7 %copy-start.9 = (f32[128,1024]{1,0:T(8,128)S(1)}, f32[128,1024]{1,0:T(8,128)}, u32[]{:S(2)}) copy-start(f32[128,1024]{1,0:T(8,128)} %get-tuple-element.192.part_ref) | copy-start | bytes 1572868
  225.2 37.7 %copy-start.10 = (f32[128,1024]{1,0:T(8,128)S(1)}, f32[128,1024]{1,0:T(8,128)}, u32[]{:S(2)}) copy-start(f32[128,1024]{1,0:T(8,128)} %get-tuple-element.193.d_residual_ref) | copy-start | bytes 1572868
  225.2 37.7 %copy-start.11 = (f32[128,128]{1,0:T(8,128)S(1)}, f32[128,128]{1,0:T(8,128)}, u32[]{:S(2)}) copy-start(f32[128,128]{1,0:T(8,128)} %get-tuple-element.167.stats_ref) | copy-start | bytes 196612
  225.2 17.9 %collective-permute-start.31 = (bf16[128,1024]{1,0:T(8,128)(2,1)S(1)}, bf16[128,1024]{1,0:T(8,128)(2,1)S(1)}, u32[]{:S(2)}, u32[]{:S(2)}) collective-permute-start(bf16[128,1024]{1,0:T(8,128)(2,1)S(1)} %get-tuple-element.189), channel_id=1, source_target_pairs={{0,2},{1,3},{2,0},{3,1},{4,6},{5,7},{6,4},{7,5},{8,10},{9,11},{10,... | collective-permute-start | bytes 786440 | tf_op jit(solution)/shard_map/ppermute | solution.py:777
  227.0 18.5 %collective-permute-start.32 = (bf16[128,1024]{1,0:T(8,128)(2,1)S(1)}, bf16[128,1024]{1,0:T(8,128)(2,1)S(1)}, u32[]{:S(2)}, u32[]{:S(2)}) collective-permute-start(bf16[128,1024]{1,0:T(8,128)(2,1)S(1)} %get-tuple-element.190), channel_id=1, source_target_pairs={{0,4},{1,5},{2,6},{3,7},{4,0},{5,1},{6,2},{7,3},{8,12},{9,13},{10,... | collective-permute-start | bytes 786440 | tf_op jit(solution)/shard_map/ppermute | solution.py:777
  228.5 23.0 %collective-permute-start.33 = (bf16[128,1024]{1,0:T(8,128)(2,1)S(1)}, bf16[128,1024]{1,0:T(8,128)(2,1)S(1)}, u32[]{:S(2)}, u32[]{:S(2)}) collective-permute-start(bf16[128,1024]{1,0:T(8,128)(2,1)S(1)} %get-tuple-element.191), channel_id=1, source_target_pairs={{0,6},{1,7},{2,4},{3,5},{4,2},{5,3},{6,0},{7,1},{8,14},{9,15},{10,... | collective-permute-start | bytes 786440 | tf_op jit(solution)/shard_map/ppermute | solution.py:777
  229.0 28.1 %collective-permute-start.27 = (bf16[128,1024]{1,0:T(8,128)(2,1)S(1)}, bf16[128,1024]{1,0:T(8,128)(2,1)S(1)}, u32[]{:S(2)}, u32[]{:S(2)}) collective-permute-start(bf16[128,1024]{1,0:T(8,128)(2,1)S(1)} %get-tuple-element.183), channel_id=1, source_target_pairs={{0,2},{1,3},{2,0},{3,1},{4,6},{5,7},{6,4},{7,5},{8,10},{9,11},{10,... | collective-permute-start | bytes 786440 | tf_op jit(solution)/shard_map/ppermute | solution.py:777
  230.8 26.3 %collective-permute-start.28 = (bf16[128,1024]{1,0:T(8,128)(2,1)S(1)}, bf16[128,1024]{1,0:T(8,128)(2,1)S(1)}, u32[]{:S(2)}, u32[]{:S(2)}) collective-permute-start(bf16[128,1024]{1,0:T(8,128)(2,1)S(1)} %get-tuple-element.184), channel_id=1, source_target_pairs={{0,4},{1,5},{2,6},{3,7},{4,0},{5,1},{6,2},{7,3},{8,12},{9,13},{10,... | collective-permute-start | bytes 786440 | tf_op jit(solution)/shard_map/ppermute | solution.py:777
  243.1 19.8 %collective-permute-start.29 = (bf16[128,1024]{1,0:T(8,128)(2,1)S(1)}, bf16[128,1024]{1,0:T(8,128)(2,1)S(1)}, u32[]{:S(2)}, u32[]{:S(2)}) collective-permute-start(bf16[128,1024]{1,0:T(8,128)(2,1)S(1)} %get-tuple-element.185), channel_id=1, source_target_pairs={{0,6},{1,7},{2,4},{3,5},{4,2},{5,3},{6,0},{7,1},{8,14},{9,15},{10,... | collective-permute-start | bytes 786440 | tf_op jit(solution)/shard_map/ppermute | solution.py:777
  (17 other events, 30.3 us)
Sparse Core Ops, SparseCore 0:
  33.1 29.1 all-gather.3
  63.9 27.4 all-gather.5
  112.3 27.1 all-gather.7
  155.3 29.2 reduce-scatter.2
  190.5 28.1 reduce-scatter.4
where the time goes:
time: 274 us; the launch traced here: 273 us
  Pallas kernels  89.3 us (33%)
  waiting for transfers between devices  80.9 us (30%)
  starting transfers between devices  65.7 us (24%)
  local copies, waits for them, and re-layouts  17.3 us (6%)
  between operations  14.3 us (5%)
  other arithmetic  5.27 us (2%)
    ppermute x31, waiting for transfers between devices, swap(): return lax.ppermute(value, 'expert', [(i, i ^ mask) for i in range(count)])  69.3 us
    ppermute x31, starting transfers between devices, swap(): return lax.ppermute(value, 'expert', [(i, i ^ mask) for i in range(count)])  28.2 us
    all_to_all x4, starting transfers between devices, team_exchange(): lax.all_to_all(value, 'expert', 0, 0, tiled=True, axis_index_groups=planes)  16.7 us
    pallas_call x1, Pallas kernels, expert(): pl.pallas_call(functools.partial(expert_kernel, chunk=chunk), in_specs=[h...  16.2 us
    all_to_all x4, starting transfers between devices, exchange(): return lax.all_to_all(value, 'expert', 0, 0, tiled=True)  14.9 us
    pallas_call x1, Pallas kernels, attend_back(): pl.pallas_call(functools.partial(attend_back_kernel, count=count), in_spe...  13.2 us
    unnamed x73, local copies, waits for them, and re-layouts  12.8 us
    pallas_call x1, Pallas kernels, feed(): pl.pallas_call(functools.partial(feed_kernel, count=count), out_shape=out...  12.4 us
  transfers between devices with their start and end apart: 47, of which 20 were waited for; matrix products, arithmetic and copies ran while one was open for 5% of the time, Pallas kernels for 32%

commit v1 on v0

--- a/solution.py
+++ b/solution.py
@@ -883,19 +883,22 @@
     )
     d_both, act = together(d_both, act)
     d_both = team_exchange(d_both)
-    narrow_grad = narrow_grads(d_out, act)
-    d_both, narrow_grad, up_grad = together(d_both, narrow_grad, up_grad)
+    d_both, up_grad = together(d_both, up_grad)
     up_grad = team_exchange(up_grad.reshape(TEAM, rows, -1))
     keep, send, grads = attend_back(
         place_arg, xs, a_near, a_far, got, joint, d_both, side, count
     )
-    grads, send, up_grad, down_grad = together(grads, send, up_grad, down_grad)
+    grads, send, up_grad, down_grad, act, *more = together(
+        grads, send, up_grad, down_grad, act, *more
+    )
     grads = exchange(grads.reshape(count, rows, -1))
     own, others = team_scatter(keep, send)
+    own, act = together(own, act)
+    narrow_grad = narrow_grads(d_out, act)
     tokens_grad, result = last(
         own, others, dense, more, result, stats, tokens, d_residual, got, count
     )
-    grads, tokens_grad = together(grads, tokens_grad)
+    grads, tokens_grad, narrow_grad = together(grads, tokens_grad, narrow_grad)
     grads = grads.reshape(teams, TEAM, rows, -1)
     joint_grad, merge_grad, up_grad, attend_grad, feed_grad, router_grad, mix_grad = owner_sums(
         grads, up_grad, width, hidden, count

time: 274 us -> 266 us (0.971)
  waiting for transfers between devices: 80.9 us -> 71.2 us
    ppermute x31, waiting for transfers between devices: 69.3 us -> 54.3 us  [swap(): return lax.ppermute(value, 'expert', [(i, i ^ mask) for i in range(count)])]
    all_to_all x4, waiting for transfers between devices: 2.93 us -> 7.11 us  [team_exchange(): lax.all_to_all(value, 'expert', 0, 0, tiled=True, axis_index_groups=planes)]
    unnamed x73 -> x79, local copies, waits for them, and re-layouts: 12.8 us -> 11.1 us
  transfers between devices with their start and end apart: 47 -> 47, of which waited for: 20 -> 19; matrix products, arithmetic and copies ran while one was open for 5% -> 5% of each run, Pallas kernels for 32% -> 33%
where the time goes in v1:
time: 266 us; the launch traced here: 265 us
  Pallas kernels  91.2 us (34%)
  waiting for transfers between devices  71.2 us (27%)
  starting transfers between devices  65.5 us (25%)
  local copies, waits for them, and re-layouts  16.3 us (6%)
  between operations  14.4 us (5%)
  other arithmetic  6.13 us (2%)
    ppermute x31, waiting for transfers between devices, swap(): return lax.ppermute(value, 'expert', [(i, i ^ mask) for i in range(count)])  54.3 us
    ppermute x31, starting transfers between devices, swap(): return lax.ppermute(value, 'expert', [(i, i ^ mask) for i in range(count)])  26.8 us
    all_to_all x4, starting transfers between devices, team_exchange(): lax.all_to_all(value, 'expert', 0, 0, tiled=True, axis_index_groups=planes)  17 us
    pallas_call x1, Pallas kernels, expert(): pl.pallas_call(functools.partial(expert_kernel, chunk=chunk), in_specs=[h...  16.2 us
    all_to_all x4, starting transfers between devices, exchange(): return lax.all_to_all(value, 'expert', 0, 0, tiled=True)  15.8 us
    pallas_call x1, Pallas kernels, attend_back(): pl.pallas_call(functools.partial(attend_back_kernel, count=count), in_spe...  13.2 us
    pallas_call x1, Pallas kernels, feed(): pl.pallas_call(functools.partial(feed_kernel, count=count), out_shape=out...  12.3 us
    unnamed x79, local copies, waits for them, and re-layouts  11.1 us
  transfers between devices with their start and end apart: 47, of which 19 were waited for; matrix products, arithmetic and copies ran while one was open for 5% of the time, Pallas kernels for 33%

profile of v1, /device:TPU:0, one launch (start us, length us, event | category | flops | bytes accessed | tf_op | source)
XLA Modules:
  0.0 264.7 jit_solution(15065759845586279375)
XLA Ops:
  7.2 2.0 pack.1
  9.2 5.3 %all-to-all-start = ((bf16[8,32,1024]{2,1,0:T(8,128)(2,1)}), bf16[8,32,1024]{2,1,0:T(8,128)(2,1)S(1)}, u32[]{:S(2)}, u32[]{:S(2)}) async-start(bf16[8,32,1024]{2,1,0:T(8,128)(2,1)} %pack.1), calls=%async_computation | async-start | bytes 1048576 | tf_op jit(solution)/shard_map/all_to_all | solution.py:783
  14.5 1.6 collective-permute-start.2
  16.1 2.6 collective-permute-start.1
  18.7 1.3 collective-permute-start
  20.0 1.4 copy.26.routes_ref
  21.4 2.5 place_rows.1
  25.0 5.2 %all-to-all-start.1 = ((bf16[32,8,1024]{2,1,0:T(8,128)(2,1)}), bf16[32,8,1024]{2,1,0:T(8,128)(2,1)S(1)}, u32[]{:S(2)}, u32[]{:S(2)}) async-start(bf16[32,8,1024]{2,1,0:T(8,128)(2,1)} %bitcast.61), calls=%async_computation.1 | async-start | bytes 1048576 | tf_op jit(solution)/shard_map/all_to_all | solution.py:780
  31.0 1.8 collective-permute-start.3
  32.9 1.5 collective-permute-start.4
  34.6 10.8 %collective-permute-done.3 = bf16[144,1024]{1,0:T(8,128)(2,1)S(1)} collective-permute-done((bf16[144,1024]{1,0:T(8,128)(2,1)S(1)}, bf16[144,1024]{1,0:T(8,128)(2,1)S(1)}, u32[]{:S(2)}, u32[]{:S(2)}) %collective-permute-start.3) | collective-permute-done | bytes 294944 | tf_op jit(solution)/shard_map/ppermute | solution.py:777
  45.6 6.6 %collective-permute-done.5 = bf16[144,1024]{1,0:T(8,128)(2,1)S(1)} collective-permute-done((bf16[144,1024]{1,0:T(8,128)(2,1)S(1)}, bf16[144,1024]{1,0:T(8,128)(2,1)S(1)}, u32[]{:S(2)}, u32[]{:S(2)}) %collective-permute-start.5) | collective-permute-done | bytes 294944 | tf_op jit(solution)/shard_map/ppermute | solution.py:777
  52.9 1.0 collective-permute-start.10
  53.8 1.5 collective-permute-start.9
  55.3 1.1 collective-permute-start.8
  57.8 4.6 %all-gather.4.cloned.1.call-done.got_ref.small_ref = bf16[1024,512]{1,0:T(8,128)(2,1)} async-done(((bf16[256,512]{1,0:T(8,128)(2,1)}), bf16[1024,512]{1,0:T(8,128)(2,1)}) %all-gather.4.cloned.1.call-update) | async-done | bytes 1048592 | tf_op jit(solution)/shard_map/all_gather | solution.py:786
  62.4 7.1 %attend.1 = (bf16[8,128,384]{2,1,0:T(8,128)(2,1)}, bf16[8,128,128]{2,1,0:T(8,128)(2,1)}) custom-call(s32[2]{0:T(128)} %pad_add_fusion.place_ref, bf16[2,144,1024]{2,1,0:T(8,128)(2,1)} %copy-done.25, bf16[2,144,1024]{2,1,0:T(8,128)(2,1)} %copy-done.26, bf16[2,144,1024]{2,1,0:T(8,128)(2,1)} %collective-permute-done.6.f0_ref, ...), custom_call_target="tpu_custom_call" | custom-call | flops 1 | bytes 1 | tf_op jit(solution)/shard_map/attend/pallas_call | solution.py:159
  69.5 1.1 pad_maximum_fusion.near_ref
  70.6 3.8 %all-to-all-start.2 = ((bf16[8,128,128]{2,1,0:T(8,128)(2,1)}), bf16[8,128,128]{2,1,0:T(8,128)(2,1)S(1)}, u32[]{:S(2)}, u32[]{:S(2)}) async-start(bf16[8,128,128]{2,1,0:T(8,128)(2,1)} %get-tuple-element.132), calls=%async_computation.2 | async-start | bytes 524288 | tf_op jit(solution)/shard_map/all_to_all | solution.py:783
  74.4 1.0 copy-done.30
  75.4 3.1 %order.1 = bf16[4,8,32,1024]{3,2,1,0:T(8,128)(2,1)} custom-call(s32[2]{0:T(128)} %pad_add_fusion.place_ref, bf16[4,128,1024]{2,1,0:T(8,128)(2,1)} %copy-done.23, bf16[4,128,1024]{2,1,0:T(8,128)(2,1)} %copy-done.30), custom_call_target="tpu_custom_call" | custom-call | flops 1 | bytes 1 | tf_op jit(solution)/shard_map/order/pallas_call | solution.py:735
  78.4 2.9 %all-to-all-done.2.att_ref = bf16[8,128,128]{2,1,0:T(8,128)(2,1)S(1)} async-done(((bf16[8,128,128]{2,1,0:T(8,128)(2,1)}), bf16[8,128,128]{2,1,0:T(8,128)(2,1)S(1)}, u32[]{:S(2)}, u32[]{:S(2)}) %all-to-all-start.2) | async-done | bytes 262176 | tf_op jit(solution)/shard_map/all_to_all | solution.py:783
  82.0 4.2 %middle.1 = (f32[128,1024]{1,0:T(8,128)}, bf16[128,1024]{1,0:T(8,128)(2,1)}, bf16[128,1024]{1,0:T(8,128)(2,1)}, f32[128,128]{1,0:T(8,128)}, bf16[256,1152]{1,0:T(8,128)(2,1)}) custom-call(bf16[8,128,128]{2,1,0:T(8,128)(2,1)} %copy-done.31, bf16[1024,1024]{1,0:T(8,128)(2,1)} %bitcast.49, bf16[128,1024]{1,0:T(8,128)(2,1)} %x_ref.1, ...), custom_call_target="tpu_custom_call" | custom-call | flops 1 | bytes 1 | tf_op jit(solution)/shard_map/middle/pallas_call | solution.py:336
  86.8 1.4 collective-permute-start.13
  88.2 1.5 collective-permute-start.12
  89.7 2.6 all-to-all-start.3
  92.4 4.2 %collective-permute-done.14 = bf16[128,1024]{1,0:T(8,128)(2,1)S(1)} collective-permute-done((bf16[128,1024]{1,0:T(8,128)(2,1)}, bf16[128,1024]{1,0:T(8,128)(2,1)S(1)}, u32[]{:S(2)}, u32[]{:S(2)}) %collective-permute-start.14) | collective-permute-done | bytes 262176 | tf_op jit(solution)/shard_map/ppermute | solution.py:777
  96.6 7.6 %collective-permute-done.13 = bf16[128,1024]{1,0:T(8,128)(2,1)S(1)} collective-permute-done((bf16[128,1024]{1,0:T(8,128)(2,1)}, bf16[128,1024]{1,0:T(8,128)(2,1)S(1)}, u32[]{:S(2)}, u32[]{:S(2)}) %collective-permute-start.13) | collective-permute-done | bytes 262176 | tf_op jit(solution)/shard_map/ppermute | solution.py:777
  104.2 1.1 pad_maximum_fusion.1.near_ref
  105.5 2.4 collective-permute-start.18
  109.9 16.2 %expert.1 = (bf16[256,4096]{1,0:T(8,128)(2,1)}, bf16[256,4096]{1,0:T(8,128)(2,1)}, bf16[256,2048]{1,0:T(8,128)(2,1)}, bf16[256,1024]{1,0:T(8,128)(2,1)}) custom-call(bf16[256,1152]{1,0:T(8,128)(2,1)} %bitcast.51, bf16[256,1024]{1,0:T(8,128)(2,1)} %bitcast.54, bf16[1,1024,4096]{2,1,0:T(8,128)(2,1)} %widen_hbm.1, bf16[1,4096,1024]{2,1,0:T(8,128)(2,1)} %narrow_hbm.1), custom_call_target="tpu_custom_call" | custom-call | flops 1 | bytes 1 | tf_op jit(solution)/shard_map/expert/pallas_call | solution.py:400
  126.1 6.0 %collective-permute-done.17 = bf16[256,1024]{1,0:T(8,128)(2,1)} collective-permute-done((bf16[256,1024]{1,0:T(8,128)(2,1)S(1)}, bf16[256,1024]{1,0:T(8,128)(2,1)}, u32[]{:S(2)}, u32[]{:S(2)}) %collective-permute-start.17) | collective-permute-done | bytes 524320 | tf_op jit(solution)/shard_map/ppermute | solution.py:777
  132.1 1.9 slice_bitcast_fusion.2
  134.0 1.9 slice_bitcast_fusion
  136.2 3.8 %all-to-all-start.4 = ((bf16[32,8,2048]{2,1,0:T(8,128)(2,1)}), bf16[32,8,2048]{2,1,0:T(8,128)(2,1)S(1)}, u32[]{:S(2)}, u32[]{:S(2)}) async-start(bf16[32,8,2048]{2,1,0:T(8,128)(2,1)} %bitcast.58), calls=%async_computation.4 | async-start | bytes 2097152 | tf_op jit(solution)/shard_map/all_to_all | solution.py:780
  140.2 0.9 copy-done.29
  141.1 12.3 %feed.1 = (f32[4,128,1152]{2,1,0:T(8,128)}, bf16[4,128,512]{2,1,0:T(8,128)(2,1)}, bf16[4,128,640]{2,1,0:T(8,128)(2,1)}, f32[4,128,1024]{2,1,0:T(8,128)}, bf16[4,...) custom-call(bf16[4,128,1024]{2,1,0:T(8,128)(2,1)} %copy-done.21, ...), custom_call_target="tpu_custom_call" | custom-call | flops 1 | bytes 1 | tf_op jit(solution)/shard_map/feed/pallas_call | solution.py:520
  154.0 2.5 collective-permute-done.21.refs_0_
  156.6 1.7 copy-done.1
  159.6 2.2 pad_maximum_fusion.2.near_att
  162.1 1.8 collective-permute-start.23
  163.8 1.5 collective-permute-start.24
  165.6 9.7 %widen_grads.1 = f32[1,1024,4096]{2,1,0:T(8,128)} custom-call(bf16[256,1152]{1,0:T(8,128)(2,1)} %bitcast.52, bf16[256,4096]{1,0:T(8,128)(2,1)} %get-tuple-element.170.d_ref), custom_call_target="tpu_custom_call" | custom-call | flops 1 | bytes 1 | tf_op jit(solution)/shard_map/widen_grads/pallas_call | solution.py:453
  175.3 3.9 %collective-permute-done.24.r2_ref = bf16[128,1152]{1,0:T(8,128)(2,1)} collective-permute-done((bf16[128,1152]{1,0:T(8,128)(2,1)S(1)}, bf16[128,1152]{1,0:T(8,128)(2,1)}, u32[]{:S(2)}, u32[]{:S(2)}) %collective-permute-start.24) | collective-permute-done | bytes 294944 | tf_op jit(solution)/shard_map/ppermute | solution.py:777
  179.2 5.7 %after.1 = (f32[128,1024]{1,0:T(8,128)}, f32[128,1024]{1,0:T(8,128)}, f32[1024,128]{1,0:T(8,128)}, bf16[8,256,128]{2,1,0:T(8,128)(2,1)}) custom-call(f32[128,1152]{1,0:T(8,128)} %copy-done.8, bf16[128,1152]{1,0:T(8,128)(2,1)} %copy-done.32, bf16[128,1152]{1,0:T(8,128)(2,1)} %collective-permute-done.24.r2_ref, ...), custom_call_target="tpu_custom_call" | custom-call | flops 1 | bytes 1 | tf_op jit(solution)/shard_map/after/pallas_call | solution.py:616
  184.9 4.3 %all-to-all-start.5 = ((bf16[8,256,128]{2,1,0:T(8,128)(2,1)}), bf16[8,256,128]{2,1,0:T(8,128)(2,1)}, u32[]{:S(2)}, u32[]{:S(2)}) async-start(bf16[8,256,128]{2,1,0:T(8,128)(2,1)} %get-tuple-element.176), calls=%async_computation.5 | async-start | bytes 1048576 | tf_op jit(solution)/shard_map/all_to_all | solution.py:783
  189.8 1.1 halve.4
  191.7 1.9 collective-permute-start.27
  193.6 1.5 collective-permute-start.28
  195.2 4.2 %all-to-all-done.5.d_ref = bf16[8,256,128]{2,1,0:T(8,128)(2,1)} async-done(((bf16[8,256,128]{2,1,0:T(8,128)(2,1)}), bf16[8,256,128]{2,1,0:T(8,128)(2,1)}, u32[]{:S(2)}, u32[]{:S(2)}) %all-to-all-start.5) | async-done | bytes 524320 | tf_op jit(solution)/shard_map/all_to_all | solution.py:783
  199.4 3.6 %all-to-all-start.6 = ((bf16[8,32,512]{2,1,0:T(8,128)(2,1)}), bf16[8,32,512]{2,1,0:T(8,128)(2,1)S(1)}, u32[]{:S(2)}, u32[]{:S(2)}) async-start(bf16[8,32,512]{2,1,0:T(8,128)(2,1)} %bitcast.66), calls=%async_computation.7 | async-start | bytes 524288 | tf_op jit(solution)/shard_map/all_to_all | solution.py:783
  203.0 13.2 %attend_back.1 = (f32[4,128,1024]{2,1,0:T(8,128)}, bf16[4,128,1024]{2,1,0:T(8,128)(2,1)}, bf16[1024,640]{1,0:T(8,128)(2,1)}) custom-call(s32[2]{0:T(128)} %pad_add_fusion.place_ref, bf16[2,144,1024]{2,1,0:T(8,128)(2,1)} %copy-done.25, bf16[2,144,1024]{2,1,0:T(8,128)(2,1)} %copy-done.26, bf16[2,144,1024]{2,1,0:T(8,128)(2,1)} %collective-permute-done.6.f0_ref, ...), custom_call_target="tpu_custom_call" | custom-call | flops 20000000000 | bytes 1 | tf_op jit(solution)/shard_map/attend_back/pallas_call | solution.py:242
  219.1 1.4 reduce-scatter.5.cloned.1.call-done
  220.5 4.2 %all-to-all-start.7 = ((bf16[32,32,640]{2,1,0:T(8,128)(2,1)}), bf16[32,32,640]{2,1,0:T(8,128)(2,1)S(1)}, u32[]{:S(2)}, u32[]{:S(2)}) async-start(bf16[32,32,640]{2,1,0:T(8,128)(2,1)} %bitcast.57), calls=%async_computation.9 | async-start | bytes 2621440 | tf_op jit(solution)/shard_map/all_to_all | solution.py:780
  225.1 2.6 collective-permute-done.30.refs_0_
  227.7 1.1 halve.5
  228.8 1.8 collective-permute-start.31
  230.6 1.5 collective-permute-start.32
  233.2 9.6 %narrow_grads.1 = f32[1,4096,1024]{2,1,0:T(8,128)} custom-call(bf16[256,1024]{1,0:T(8,128)(2,1)} %get-tuple-element.207.rows_ref, bf16[256,4096]{1,0:T(8,128)(2,1)} %get-tuple-element.208.act_ref), custom_call_target="tpu_custom_call" | custom-call | flops 1 | bytes 1 | tf_op jit(solution)/shard_map/narrow_grads/pallas_call | solution.py:431
  242.8 1.8 collective-permute-done.31.r1_ref
  245.0 7.7 %collective-permute-done.33.r3_ref = bf16[128,1024]{1,0:T(8,128)(2,1)S(1)} collective-permute-done((bf16[128,1024]{1,0:T(8,128)(2,1)}, bf16[128,1024]{1,0:T(8,128)(2,1)S(1)}, u32[]{:S(2)}, u32[]{:S(2)}) %collective-permute-start.33) | collective-permute-done | bytes 262176 | tf_op jit(solution)/shard_map/ppermute | solution.py:777
  252.8 2.2 last.1
  255.0 2.0 all-to-all-done.7
  257.0 1.2 owner_sums.1
  (146 shorter events, 17.1 us)
Async XLA Ops:
  7.2 23.8 %copy-start.36 = (s32[1,128]{1,0:T(1,128)S(1)}, s32[1,128]{1,0:T(1,128)}, u32[]{:S(2)}) copy-start(s32[1,128]{1,0:T(1,128)} %param.26) | copy-start | bytes 1540
  7.2 23.8 %copy-start.2 = (bf16[128,1024]{1,0:T(8,128)(2,1)S(1)}, bf16[128,1024]{1,0:T(8,128)(2,1)}, u32[]{:S(2)}) copy-start(bf16[128,1024]{1,0:T(8,128)(2,1)} %x_ref.1) | copy-start | bytes 786436
  9.2 25.4 %copy-start.35 = (bf16[32,1024]{1,0:T(8,128)(2,1)S(1)}, bf16[32,1024]{1,0:T(8,128)(2,1)}, u32[]{:S(2)}) copy-start(bf16[32,1024]{1,0:T(8,128)(2,1)} %param.17) | copy-start | bytes 196612
  9.2 15.0 %all-to-all-start = ((bf16[8,32,1024]{2,1,0:T(8,128)(2,1)}), bf16[8,32,1024]{2,1,0:T(8,128)(2,1)S(1)}, u32[]{:S(2)}, u32[]{:S(2)}) async-start(bf16[8,32,1024]{2,1,0:T(8,128)(2,1)} %pack.1), calls=%async_computation | async-start | bytes 1048576 | tf_op jit(solution)/shard_map/all_to_all | solution.py:783
  14.5 9.4 %collective-permute-start.2 = (bf16[32,1024]{1,0:T(8,128)(2,1)}, bf16[32,1024]{1,0:T(8,128)(2,1)S(1)}, u32[]{:S(2)}, u32[]{:S(2)}) collective-permute-start(bf16[32,1024]{1,0:T(8,128)(2,1)} %param.17), channel_id=1, source_target_pairs={{24,0},{25,1},{26,2},{27,3},{28,4},{29,5},{30,6},{31,7},{0,8},{1,9... | collective-permute-start | bytes 196616 | tf_op jit(solution)/shard_map/ppermute | solution.py:830
  16.1 7.9 %collective-permute-start.1 = (bf16[32,1024]{1,0:T(8,128)(2,1)}, bf16[32,1024]{1,0:T(8,128)(2,1)S(1)}, u32[]{:S(2)}, u32[]{:S(2)}) collective-permute-start(bf16[32,1024]{1,0:T(8,128)(2,1)} %param.17), channel_id=1, source_target_pairs={{16,0},{17,1},{18,2},{19,3},{20,4},{21,5},{22,6},{23,7},{24,8},{25... | collective-permute-start | bytes 196616 | tf_op jit(solution)/shard_map/ppermute | solution.py:830
  18.7 5.6 %collective-permute-start = (bf16[32,1024]{1,0:T(8,128)(2,1)}, bf16[32,1024]{1,0:T(8,128)(2,1)S(1)}, u32[]{:S(2)}, u32[]{:S(2)}) collective-permute-start(bf16[32,1024]{1,0:T(8,128)(2,1)} %param.17), channel_id=1, source_target_pairs={{8,0},{9,1},{10,2},{11,3},{12,4},{13,5},{14,6},{15,7},{16,8},{17,9... | collective-permute-start | bytes 196616 | tf_op jit(solution)/shard_map/ppermute | solution.py:830
  25.0 27.3 %all-to-all-start.1 = ((bf16[32,8,1024]{2,1,0:T(8,128)(2,1)}), bf16[32,8,1024]{2,1,0:T(8,128)(2,1)S(1)}, u32[]{:S(2)}, u32[]{:S(2)}) async-start(bf16[32,8,1024]{2,1,0:T(8,128)(2,1)} %bitcast.61), calls=%async_computation.1 | async-start | bytes 1048576 | tf_op jit(solution)/shard_map/all_to_all | solution.py:780
  30.2 32.2 %all-gather.4.cloned.1.call-start = ((), (), s32[]{:S(2)}) async-start(), calls=%async_computation.10 | async-start | bytes 1310720 | tf_op jit(solution)/shard_map/all_gather | solution.py:786
  30.9 74.5 %all-gather.6.cloned.1.call-start = ((), (), s32[]{:S(2)}) async-start(), calls=%async_computation.11 | async-start | bytes 1310720 | tf_op jit(solution)/shard_map/all_gather | solution.py:786
  31.0 14.3 %collective-permute-start.3 = (bf16[144,1024]{1,0:T(8,128)(2,1)S(1)}, bf16[144,1024]{1,0:T(8,128)(2,1)S(1)}, u32[]{:S(2)}, u32[]{:S(2)}) collective-permute-start(bf16[144,1024]{1,0:T(8,128)(2,1)S(1)} %get-tuple-element.231), channel_id=1, source_target_pairs={{0,2},{1,3},{2,0},{3,1},{4,6},{5,7},{6,4},{7,5},{8,10},{9,11},{10,... | collective-permute-start | bytes 884744 | tf_op jit(solution)/shard_map/ppermute | solution.py:777
  32.9 12.7 %collective-permute-start.4 = (bf16[144,1024]{1,0:T(8,128)(2,1)S(1)}, bf16[144,1024]{1,0:T(8,128)(2,1)S(1)}, u32[]{:S(2)}, u32[]{:S(2)}) collective-permute-start(bf16[144,1024]{1,0:T(8,128)(2,1)S(1)} %get-tuple-element.231), channel_id=1, source_target_pairs={{0,4},{1,5},{2,6},{3,7},{4,0},{5,1},{6,2},{7,3},{8,12},{9,13},{10,... | collective-permute-start | bytes 884744 | tf_op jit(solution)/shard_map/ppermute | solution.py:777
  34.3 17.8 %collective-permute-start.5 = (bf16[144,1024]{1,0:T(8,128)(2,1)S(1)}, bf16[144,1024]{1,0:T(8,128)(2,1)S(1)}, u32[]{:S(2)}, u32[]{:S(2)}) collective-permute-start(bf16[144,1024]{1,0:T(8,128)(2,1)S(1)} %get-tuple-element.231), channel_id=1, source_target_pairs={{0,6},{1,7},{2,4},{3,5},{4,2},{5,3},{6,0},{7,1},{8,14},{9,15},{10,... | collective-permute-start | bytes 884744 | tf_op jit(solution)/shard_map/ppermute | solution.py:777
  45.4 16.9 %copy-start.25 = (bf16[2,144,1024]{2,1,0:T(8,128)(2,1)}, bf16[2,144,1024]{2,1,0:T(8,128)(2,1)S(1)}, u32[]{:S(2)}) copy-start(bf16[2,144,1024]{2,1,0:T(8,128)(2,1)S(1)} %pad_maximum_fusion.4.n0_ref) | copy-start | bytes 1769476
  52.3 17.2 %copy-start.28 = (bf16[32,8,1024]{2,1,0:T(8,128)(2,1)}, bf16[32,8,1024]{2,1,0:T(8,128)(2,1)S(1)}, u32[]{:S(2)}) copy-start(bf16[32,8,1024]{2,1,0:T(8,128)(2,1)S(1)} %all-to-all-done.1) | copy-start | bytes 1572868
  52.3 10.1 %collective-permute-start.6 = (bf16[2,144,1024]{2,1,0:T(8,128)(2,1)S(1)}, bf16[2,144,1024]{2,1,0:T(8,128)(2,1)}, u32[]{:S(2)}, u32[]{:S(2)}) collective-permute-start(bf16[2,144,1024]{2,1,0:T(8,128)(2,1)S(1)} %pad_maximum_fusion.4.n0_ref), channel_id=1, source_target_pairs={{0,1},{1,0},{2,3},{3,2},{4,5},{5,4},{6,7},{7,6},{8,9},{9,8},{10,11... | collective-permute-start | bytes 1769480 | tf_op jit(solution)/shard_map/ppermute | solution.py:777
  52.3 10.0 %collective-permute-start.7 = (bf16[2,144,1024]{2,1,0:T(8,128)(2,1)S(1)}, bf16[2,144,1024]{2,1,0:T(8,128)(2,1)}, u32[]{:S(2)}, u32[]{:S(2)}) collective-permute-start(bf16[2,144,1024]{2,1,0:T(8,128)(2,1)S(1)} %pad_maximum_fusion.5.n1_ref), channel_id=1, source_target_pairs={{0,1},{1,0},{2,3},{3,2},{4,5},{5,4},{6,7},{7,6},{8,9},{9,8},{10,11... | collective-permute-start | bytes 1769480 | tf_op jit(solution)/shard_map/ppermute | solution.py:777
  52.9 16.6 %collective-permute-start.10 = (bf16[128,1024]{1,0:T(8,128)(2,1)S(1)}, bf16[128,1024]{1,0:T(8,128)(2,1)S(1)}, u32[]{:S(2)}, u32[]{:S(2)}) collective-permute-start(bf16[128,1024]{1,0:T(8,128)(2,1)S(1)} %constant_dynamic-update-slice_fusion), channel_id=1, source_target_pairs={{0,6},{1,7},{2,4},{3,5},{4,2},{5,3},{6,0},{7,1},{8,14},{9,15},{10,... | collective-permute-start | bytes 786440 | tf_op jit(solution)/shard_map/ppermute | solution.py:777
  53.8 15.6 %collective-permute-start.9 = (bf16[128,1024]{1,0:T(8,128)(2,1)S(1)}, bf16[128,1024]{1,0:T(8,128)(2,1)S(1)}, u32[]{:S(2)}, u32[]{:S(2)}) collective-permute-start(bf16[128,1024]{1,0:T(8,128)(2,1)S(1)} %constant_dynamic-update-slice_fusion), channel_id=1, source_target_pairs={{0,4},{1,5},{2,6},{3,7},{4,0},{5,1},{6,2},{7,3},{8,12},{9,13},{10,... | collective-permute-start | bytes 786440 | tf_op jit(solution)/shard_map/ppermute | solution.py:777
  55.3 14.1 %collective-permute-start.8 = (bf16[128,1024]{1,0:T(8,128)(2,1)S(1)}, bf16[128,1024]{1,0:T(8,128)(2,1)}, u32[]{:S(2)}, u32[]{:S(2)}) collective-permute-start(bf16[128,1024]{1,0:T(8,128)(2,1)S(1)} %constant_dynamic-update-slice_fusion), channel_id=1, source_target_pairs={{0,2},{1,3},{2,0},{3,1},{4,6},{5,7},{6,4},{7,5},{8,10},{9,11},{10,... | collective-permute-start | bytes 786440 | tf_op jit(solution)/shard_map/ppermute | solution.py:777
  70.6 3.8 %collective-permute-start.11 = (bf16[4,128,1024]{2,1,0:T(8,128)(2,1)S(1)}, bf16[4,128,1024]{2,1,0:T(8,128)(2,1)S(1)}, u32[]{:S(2)}, u32[]{:S(2)}) collective-permute-start(bf16[4,128,1024]{2,1,0:T(8,128)(2,1)S(1)} %pad_maximum_fusion.near_ref), channel_id=1, source_target_pairs={{0,1},{1,0},{2,3},{3,2},{4,5},{5,4},{6,7},{7,6},{8,9},{9,8},{10,11... | collective-permute-start | bytes 3145736 | tf_op jit(solution)/shard_map/ppermute | solution.py:777
  70.6 10.7 %all-to-all-start.2 = ((bf16[8,128,128]{2,1,0:T(8,128)(2,1)}), bf16[8,128,128]{2,1,0:T(8,128)(2,1)S(1)}, u32[]{:S(2)}, u32[]{:S(2)}) async-start(bf16[8,128,128]{2,1,0:T(8,128)(2,1)} %get-tuple-element.132), calls=%async_computation.2 | async-start | bytes 524288 | tf_op jit(solution)/shard_map/all_to_all | solution.py:783
  86.2 19.2 %copy-start.34 = (bf16[128,1024]{1,0:T(8,128)(2,1)S(1)}, bf16[128,1024]{1,0:T(8,128)(2,1)}, u32[]{:S(2)}) copy-start(bf16[128,1024]{1,0:T(8,128)(2,1)} %get-tuple-element.148) | copy-start | bytes 786436
  86.2 19.3 %copy-start.27 = (bf16[128,1024]{1,0:T(8,128)(2,1)S(1)}, bf16[128,1024]{1,0:T(8,128)(2,1)}, u32[]{:S(2)}) copy-start(bf16[128,1024]{1,0:T(8,128)(2,1)} %g_ref.3) | copy-start | bytes 786436
  86.2 10.4 %collective-permute-start.14 = (bf16[128,1024]{1,0:T(8,128)(2,1)}, bf16[128,1024]{1,0:T(8,128)(2,1)S(1)}, u32[]{:S(2)}, u32[]{:S(2)}) collective-permute-start(bf16[128,1024]{1,0:T(8,128)(2,1)} %get-tuple-element.139.second_ref), channel_id=1, source_target_pairs={{0,6},{1,7},{2,4},{3,5},{4,2},{5,3},{6,0},{7,1},{8,14},{9,15},{10,... | collective-permute-start | bytes 786440 | tf_op jit(solution)/shard_map/ppermute | solution.py:777
  86.8 17.5 %collective-permute-start.13 = (bf16[128,1024]{1,0:T(8,128)(2,1)}, bf16[128,1024]{1,0:T(8,128)(2,1)S(1)}, u32[]{:S(2)}, u32[]{:S(2)}) collective-permute-start(bf16[128,1024]{1,0:T(8,128)(2,1)} %get-tuple-element.139.second_ref), channel_id=1, source_target_pairs={{0,4},{1,5},{2,6},{3,7},{4,0},{5,1},{6,2},{7,3},{8,12},{9,13},{10,... | collective-permute-start | bytes 786440 | tf_op jit(solution)/shard_map/ppermute | solution.py:777
  88.2 16.0 %collective-permute-start.12 = (bf16[128,1024]{1,0:T(8,128)(2,1)}, bf16[128,1024]{1,0:T(8,128)(2,1)S(1)}, u32[]{:S(2)}, u32[]{:S(2)}) collective-permute-start(bf16[128,1024]{1,0:T(8,128)(2,1)} %get-tuple-element.139.second_ref), channel_id=1, source_target_pairs={{0,2},{1,3},{2,0},{3,1},{4,6},{5,7},{6,4},{7,5},{8,10},{9,11},{10,... | collective-permute-start | bytes 786440 | tf_op jit(solution)/shard_map/ppermute | solution.py:777
  89.7 19.4 %all-to-all-start.3 = ((bf16[32,8,1152]{2,1,0:T(8,128)(2,1)}), bf16[32,8,1152]{2,1,0:T(8,128)(2,1)S(1)}, u32[]{:S(2)}, u32[]{:S(2)}) async-start(bf16[32,8,1152]{2,1,0:T(8,128)(2,1)} %bitcast.60), calls=%async_computation.3 | async-start | bytes 1179648 | tf_op jit(solution)/shard_map/all_to_all | solution.py:780
  92.3 47.9 %all-gather.8.cloned.1.call-start = ((), (), s32[]{:S(2)}) async-start(), calls=%async_computation.12 | async-start | bytes 1310720 | tf_op jit(solution)/shard_map/all_gather | solution.py:786
  105.3 20.8 %copy-start.21 = (bf16[4,128,1024]{2,1,0:T(8,128)(2,1)}, bf16[4,128,1024]{2,1,0:T(8,128)(2,1)S(1)}, u32[]{:S(2)}) copy-start(bf16[4,128,1024]{2,1,0:T(8,128)(2,1)S(1)} %pad_maximum_fusion.1.near_ref) | copy-start | bytes 3145732
  105.4 3.7 %collective-permute-start.15 = (bf16[4,128,1024]{2,1,0:T(8,128)(2,1)S(1)}, bf16[4,128,1024]{2,1,0:T(8,128)(2,1)}, u32[]{:S(2)}, u32[]{:S(2)}) collective-permute-start(bf16[4,128,1024]{2,1,0:T(8,128)(2,1)S(1)} %pad_maximum_fusion.1.near_ref), channel_id=1, source_target_pairs={{0,1},{1,0},{2,3},{3,2},{4,5},{5,4},{6,7},{7,6},{8,9},{9,8},{10,11... | collective-permute-start | bytes 3145736 | tf_op jit(solution)/shard_map/ppermute | solution.py:777
  105.5 20.6 %collective-permute-start.18 = (bf16[256,1024]{1,0:T(8,128)(2,1)S(1)}, bf16[256,1024]{1,0:T(8,128)(2,1)S(1)}, u32[]{:S(2)}, u32[]{:S(2)}) collective-permute-start(bf16[256,1024]{1,0:T(8,128)(2,1)S(1)} %constant_dynamic-update-slice_fusion.4), channel_id=1, source_target_pairs={{0,6},{1,7},{2,4},{3,5},{4,2},{5,3},{6,0},{7,1},{8,14},{9,15},{10,... | collective-permute-start | bytes 1572872 | tf_op jit(solution)/shard_map/ppermute | solution.py:777
  107.9 24.3 %collective-permute-start.17 = (bf16[256,1024]{1,0:T(8,128)(2,1)S(1)}, bf16[256,1024]{1,0:T(8,128)(2,1)}, u32[]{:S(2)}, u32[]{:S(2)}) collective-permute-start(bf16[256,1024]{1,0:T(8,128)(2,1)S(1)} %constant_dynamic-update-slice_fusion.4), channel_id=1, source_target_pairs={{0,4},{1,5},{2,6},{3,7},{4,0},{5,1},{6,2},{7,3},{8,12},{9,13},{10,... | collective-permute-start | bytes 1572872 | tf_op jit(solution)/shard_map/ppermute | solution.py:777
  108.2 23.9 %collective-permute-start.16 = (bf16[256,1024]{1,0:T(8,128)(2,1)S(1)}, bf16[256,1024]{1,0:T(8,128)(2,1)}, u32[]{:S(2)}, u32[]{:S(2)}) collective-permute-start(bf16[256,1024]{1,0:T(8,128)(2,1)S(1)} %constant_dynamic-update-slice_fusion.4), channel_id=1, source_target_pairs={{0,2},{1,3},{2,0},{3,1},{4,6},{5,7},{6,4},{7,5},{8,10},{9,11},{10,... | collective-permute-start | bytes 1572872 | tf_op jit(solution)/shard_map/ppermute | solution.py:777
  136.0 4.1 %collective-permute-start.20 = (bf16[4,128,1024]{2,1,0:T(8,128)(2,1)S(1)}, bf16[4,128,1024]{2,1,0:T(8,128)(2,1)S(1)}, u32[]{:S(2)}, u32[]{:S(2)}) collective-permute-start(bf16[4,128,1024]{2,1,0:T(8,128)(2,1)S(1)} %pad_maximum_fusion.3.g_near_ref), channel_id=1, source_target_pairs={{0,1},{1,0},{2,3},{3,2},{4,5},{5,4},{6,7},{7,6},{8,9},{9,8},{10,11... | collective-permute-start | bytes 3145736 | tf_op jit(solution)/shard_map/ppermute | solution.py:777
  136.2 39.1 %all-to-all-start.4 = ((bf16[32,8,2048]{2,1,0:T(8,128)(2,1)}), bf16[32,8,2048]{2,1,0:T(8,128)(2,1)S(1)}, u32[]{:S(2)}, u32[]{:S(2)}) async-start(bf16[32,8,2048]{2,1,0:T(8,128)(2,1)} %bitcast.58), calls=%async_computation.4 | async-start | bytes 2097152 | tf_op jit(solution)/shard_map/all_to_all | solution.py:780
  139.9 59.5 %reduce-scatter.3.cloned.1.call-start = ((), (), s32[]{:S(2)}) async-start(), calls=%async_computation.13 | async-start | bytes 1310720 | tf_op jit(solution)/shard_map/reduce_scatter | solution.py:789
  153.5 3.1 %collective-permute-start.22 = (bf16[4,128,640]{2,1,0:T(8,128)(2,1)}, bf16[4,128,640]{2,1,0:T(8,128)(2,1)S(1)}, u32[]{:S(2)}, u32[]{:S(2)}) collective-permute-start(bf16[4,128,640]{2,1,0:T(8,128)(2,1)} %get-tuple-element.160), channel_id=1, source_target_pairs={{0,1},{1,0},{2,3},{3,2},{4,5},{5,4},{6,7},{7,6},{8,9},{9,8},{10,11... | collective-permute-start | bytes 1966088 | tf_op jit(solution)/shard_map/ppermute | solution.py:777
  153.8 2.8 %collective-permute-start.21 = (bf16[4,128,512]{2,1,0:T(8,128)(2,1)}, bf16[4,128,512]{2,1,0:T(8,128)(2,1)S(1)}, u32[]{:S(2)}, u32[]{:S(2)}) collective-permute-start(bf16[4,128,512]{2,1,0:T(8,128)(2,1)} %get-tuple-element.159), channel_id=1, source_target_pairs={{0,1},{1,0},{2,3},{3,2},{4,5},{5,4},{6,7},{7,6},{8,9},{9,8},{10,11... | collective-permute-start | bytes 1572872 | tf_op jit(solution)/shard_map/ppermute | solution.py:777
  159.3 30.4 %collective-permute-start.26 = (bf16[4,128,1024]{2,1,0:T(8,128)(2,1)}, bf16[4,128,1024]{2,1,0:T(8,128)(2,1)S(1)}, u32[]{:S(2)}, u32[]{:S(2)}) collective-permute-start(bf16[4,128,1024]{2,1,0:T(8,128)(2,1)} %get-tuple-element.187), channel_id=1, source_target_pairs={{0,1},{1,0},{2,3},{3,2},{4,5},{5,4},{6,7},{7,6},{8,9},{9,8},{10,11... | collective-permute-start | bytes 3145736 | tf_op jit(solution)/shard_map/ppermute | solution.py:777
  161.8 41.2 %collective-permute-start.19 = (bf16[4,128,1024]{2,1,0:T(8,128)(2,1)}, bf16[4,128,1024]{2,1,0:T(8,128)(2,1)}, u32[]{:S(2)}, u32[]{:S(2)}) collective-permute-start(bf16[4,128,1024]{2,1,0:T(8,128)(2,1)} %pad_maximum_fusion.2.near_att), channel_id=1, source_target_pairs={{0,1},{1,0},{2,3},{3,2},{4,5},{5,4},{6,7},{7,6},{8,9},{9,8},{10,11... | collective-permute-start | bytes 3145736 | tf_op jit(solution)/shard_map/ppermute | solution.py:777
  162.1 13.2 %collective-permute-start.23 = (bf16[128,1152]{1,0:T(8,128)(2,1)S(1)}, bf16[128,1152]{1,0:T(8,128)(2,1)S(1)}, u32[]{:S(2)}, u32[]{:S(2)}) collective-permute-start(bf16[128,1152]{1,0:T(8,128)(2,1)S(1)} %get-tuple-element.166), channel_id=1, source_target_pairs={{0,2},{1,3},{2,0},{3,1},{4,6},{5,7},{6,4},{7,5},{8,10},{9,11},{10,... | collective-permute-start | bytes 884744 | tf_op jit(solution)/shard_map/ppermute | solution.py:777
  163.8 15.3 %collective-permute-start.24 = (bf16[128,1152]{1,0:T(8,128)(2,1)S(1)}, bf16[128,1152]{1,0:T(8,128)(2,1)}, u32[]{:S(2)}, u32[]{:S(2)}) collective-permute-start(bf16[128,1152]{1,0:T(8,128)(2,1)S(1)} %get-tuple-element.167), channel_id=1, source_target_pairs={{0,4},{1,5},{2,6},{3,7},{4,0},{5,1},{6,2},{7,3},{8,12},{9,13},{10,... | collective-permute-start | bytes 884744 | tf_op jit(solution)/shard_map/ppermute | solution.py:777
  165.3 13.8 %collective-permute-start.25 = (bf16[128,1152]{1,0:T(8,128)(2,1)S(1)}, bf16[128,1152]{1,0:T(8,128)(2,1)}, u32[]{:S(2)}, u32[]{:S(2)}) collective-permute-start(bf16[128,1152]{1,0:T(8,128)(2,1)S(1)} %get-tuple-element.168), channel_id=1, source_target_pairs={{0,6},{1,7},{2,4},{3,5},{4,2},{5,3},{6,0},{7,1},{8,14},{9,15},{10,... | collective-permute-start | bytes 884744 | tf_op jit(solution)/shard_map/ppermute | solution.py:777
  184.9 14.5 %all-to-all-start.5 = ((bf16[8,256,128]{2,1,0:T(8,128)(2,1)}), bf16[8,256,128]{2,1,0:T(8,128)(2,1)}, u32[]{:S(2)}, u32[]{:S(2)}) async-start(bf16[8,256,128]{2,1,0:T(8,128)(2,1)} %get-tuple-element.176), calls=%async_computation.5 | async-start | bytes 1048576 | tf_op jit(solution)/shard_map/all_to_all | solution.py:783
  189.2 31.4 %reduce-scatter.5.cloned.1.call-start = ((), (), s32[]{:S(2)}) async-start(), calls=%async_computation.14 | async-start | bytes 1310720 | tf_op jit(solution)/shard_map/reduce_scatter | solution.py:789
  191.7 24.5 %collective-permute-start.27 = (bf16[128,1024]{1,0:T(8,128)(2,1)}, bf16[128,1024]{1,0:T(8,128)(2,1)S(1)}, u32[]{:S(2)}, u32[]{:S(2)}) collective-permute-start(bf16[128,1024]{1,0:T(8,128)(2,1)} %get-tuple-element.188), channel_id=1, source_target_pairs={{0,2},{1,3},{2,0},{3,1},{4,6},{5,7},{6,4},{7,5},{8,10},{9,11},{10,... | collective-permute-start | bytes 786440 | tf_op jit(solution)/shard_map/ppermute | solution.py:777
  193.6 23.4 %collective-permute-start.28 = (bf16[128,1024]{1,0:T(8,128)(2,1)}, bf16[128,1024]{1,0:T(8,128)(2,1)S(1)}, u32[]{:S(2)}, u32[]{:S(2)}) collective-permute-start(bf16[128,1024]{1,0:T(8,128)(2,1)} %get-tuple-element.189), channel_id=1, source_target_pairs={{0,4},{1,5},{2,6},{3,7},{4,0},{5,1},{6,2},{7,3},{8,12},{9,13},{10,... | collective-permute-start | bytes 786440 | tf_op jit(solution)/shard_map/ppermute | solution.py:777
  195.1 22.6 %collective-permute-start.29 = (bf16[128,1024]{1,0:T(8,128)(2,1)}, bf16[128,1024]{1,0:T(8,128)(2,1)S(1)}, u32[]{:S(2)}, u32[]{:S(2)}) collective-permute-start(bf16[128,1024]{1,0:T(8,128)(2,1)} %get-tuple-element.190), channel_id=1, source_target_pairs={{0,6},{1,7},{2,4},{3,5},{4,2},{5,3},{6,0},{7,1},{8,14},{9,15},{10,... | collective-permute-start | bytes 786440 | tf_op jit(solution)/shard_map/ppermute | solution.py:777
  199.4 19.0 %all-to-all-start.6 = ((bf16[8,32,512]{2,1,0:T(8,128)(2,1)}), bf16[8,32,512]{2,1,0:T(8,128)(2,1)S(1)}, u32[]{:S(2)}, u32[]{:S(2)}) async-start(bf16[8,32,512]{2,1,0:T(8,128)(2,1)} %bitcast.66), calls=%async_computation.7 | async-start | bytes 524288 | tf_op jit(solution)/shard_map/all_to_all | solution.py:783
  220.5 36.5 %all-to-all-start.7 = ((bf16[32,32,640]{2,1,0:T(8,128)(2,1)}), bf16[32,32,640]{2,1,0:T(8,128)(2,1)S(1)}, u32[]{:S(2)}, u32[]{:S(2)}) async-start(bf16[32,32,640]{2,1,0:T(8,128)(2,1)} %bitcast.57), calls=%async_computation.9 | async-start | bytes 2621440 | tf_op jit(solution)/shard_map/all_to_all | solution.py:780
  224.8 2.9 %collective-permute-start.30 = (bf16[4,128,1024]{2,1,0:T(8,128)(2,1)}, bf16[4,128,1024]{2,1,0:T(8,128)(2,1)S(1)}, u32[]{:S(2)}, u32[]{:S(2)}) collective-permute-start(bf16[4,128,1024]{2,1,0:T(8,128)(2,1)} %get-tuple-element.191), channel_id=1, source_target_pairs={{0,1},{1,0},{2,3},{3,2},{4,5},{5,4},{6,7},{7,6},{8,9},{9,8},{10,11... | collective-permute-start | bytes 3145736 | tf_op jit(solution)/shard_map/ppermute | solution.py:777
  228.8 15.8 %collective-permute-start.31 = (bf16[128,1024]{1,0:T(8,128)(2,1)}, bf16[128,1024]{1,0:T(8,128)(2,1)S(1)}, u32[]{:S(2)}, u32[]{:S(2)}) collective-permute-start(bf16[128,1024]{1,0:T(8,128)(2,1)} %get-tuple-element.195), channel_id=1, source_target_pairs={{0,2},{1,3},{2,0},{3,1},{4,6},{5,7},{6,4},{7,5},{8,10},{9,11},{10,... | collective-permute-start | bytes 786440 | tf_op jit(solution)/shard_map/ppermute | solution.py:777
  230.6 14.4 %collective-permute-start.32 = (bf16[128,1024]{1,0:T(8,128)(2,1)}, bf16[128,1024]{1,0:T(8,128)(2,1)S(1)}, u32[]{:S(2)}, u32[]{:S(2)}) collective-permute-start(bf16[128,1024]{1,0:T(8,128)(2,1)} %get-tuple-element.196), channel_id=1, source_target_pairs={{0,4},{1,5},{2,6},{3,7},{4,0},{5,1},{6,2},{7,3},{8,12},{9,13},{10,... | collective-permute-start | bytes 786440 | tf_op jit(solution)/shard_map/ppermute | solution.py:777
  232.0 20.7 %collective-permute-start.33 = (bf16[128,1024]{1,0:T(8,128)(2,1)}, bf16[128,1024]{1,0:T(8,128)(2,1)S(1)}, u32[]{:S(2)}, u32[]{:S(2)}) collective-permute-start(bf16[128,1024]{1,0:T(8,128)(2,1)} %get-tuple-element.197), channel_id=1, source_target_pairs={{0,6},{1,7},{2,4},{3,5},{4,2},{5,3},{6,0},{7,1},{8,14},{9,15},{10,... | collective-permute-start | bytes 786440 | tf_op jit(solution)/shard_map/ppermute | solution.py:777
  233.1 19.6 %copy-start = (bf16[1024,512]{1,0:T(8,128)(2,1)S(1)}, bf16[1024,512]{1,0:T(8,128)(2,1)}, u32[]{:S(2)}) copy-start(bf16[1024,512]{1,0:T(8,128)(2,1)} %all-gather.4.cloned.1.call-done.got_ref.small_ref) | copy-start | bytes 3145732
  233.1 19.6 %copy-start.3 = (bf16[128,1024]{1,0:T(8,128)(2,1)S(1)}, bf16[128,1024]{1,0:T(8,128)(2,1)}, u32[]{:S(2)}) copy-start(bf16[128,1024]{1,0:T(8,128)(2,1)} %x_ref.1) | copy-start | bytes 786436
  233.1 19.6 %copy-start.9 = (f32[128,1024]{1,0:T(8,128)S(1)}, f32[128,1024]{1,0:T(8,128)}, u32[]{:S(2)}) copy-start(f32[128,1024]{1,0:T(8,128)} %get-tuple-element.202.part_ref) | copy-start | bytes 1572868
  233.2 19.6 %copy-start.10 = (f32[128,1024]{1,0:T(8,128)S(1)}, f32[128,1024]{1,0:T(8,128)}, u32[]{:S(2)}) copy-start(f32[128,1024]{1,0:T(8,128)} %get-tuple-element.203.d_residual_ref) | copy-start | bytes 1572868
  233.2 19.6 %copy-start.12 = (f32[128,1024]{1,0:T(8,128)S(1)}, f32[128,1024]{1,0:T(8,128)}, u32[]{:S(2)}) copy-start(f32[128,1024]{1,0:T(8,128)} %copy-done.11) | copy-start | bytes 1572868
  233.2 19.6 %copy-start.13 = (f32[128,128]{1,0:T(8,128)S(1)}, f32[128,128]{1,0:T(8,128)}, u32[]{:S(2)}) copy-start(f32[128,128]{1,0:T(8,128)} %get-tuple-element.173.stats_ref) | copy-start | bytes 196612
  233.2 19.6 %copy-start.15 = (bf16[128,1024]{1,0:T(8,128)(2,1)S(1)}, bf16[128,1024]{1,0:T(8,128)(2,1)}, u32[]{:S(2)}) copy-start(bf16[128,1024]{1,0:T(8,128)(2,1)} %copy-done.14) | copy-start | bytes 786436
  233.2 19.6 %copy-start.17 = (bf16[128,1024]{1,0:T(8,128)(2,1)S(1)}, bf16[128,1024]{1,0:T(8,128)(2,1)}, u32[]{:S(2)}) copy-start(bf16[128,1024]{1,0:T(8,128)(2,1)} %copy-done.16) | copy-start | bytes 786436
  233.2 19.6 %copy-start.19 = (bf16[128,1024]{1,0:T(8,128)(2,1)S(1)}, bf16[128,1024]{1,0:T(8,128)(2,1)}, u32[]{:S(2)}) copy-start(bf16[128,1024]{1,0:T(8,128)(2,1)} %copy-done.18) | copy-start | bytes 786436
  (20 other events, 63.7 us)
Sparse Core Ops, SparseCore 0:
  33.1 29.1 all-gather.3
  63.9 27.4 all-gather.5
  109.2 27.1 all-gather.7
  153.6 29.4 reduce-scatter.2
  192.1 28.3 reduce-scatter.4

commit v2 on v1

--- a/solution.py
+++ b/solution.py
@@ -888,9 +888,7 @@
     keep, send, grads = attend_back(
         place_arg, xs, a_near, a_far, got, joint, d_both, side, count
     )
-    grads, send, up_grad, down_grad, act, *more = together(
-        grads, send, up_grad, down_grad, act, *more
-    )
+    grads, send, up_grad, act, *more = together(grads, send, up_grad, act, *more)
     grads = exchange(grads.reshape(count, rows, -1))
     own, others = team_scatter(keep, send)
     own, act = together(own, act)

time: 266 us -> 294 us (1.11)
  waiting for transfers between devices: 71.2 us -> 94.4 us
    reduce_scatter x2, waiting for transfers between devices: 1.43 us -> 36 us  [line_scatter(): lax.psum_scatter(value, 'expert', scatter_dimension=0, tiled=True, axis_i...]
    ppermute x31, waiting for transfers between devices: 54.3 us -> 44.4 us  [swap(): return lax.ppermute(value, 'expert', [(i, i ^ mask) for i in range(count)])]
    unnamed x79 -> x81, local copies, waits for them, and re-layouts: 11.1 us -> 11.9 us
  transfers between devices with their start and end apart: 47 -> 47, of which waited for: 19 -> 15; matrix products, arithmetic and copies ran while one was open for 5% -> 4% of each run, Pallas kernels for 33% -> 30%
where the time goes in v2:
time: 294 us; the launch traced here: 291 us
  waiting for transfers between devices  94.4 us (32%)
  Pallas kernels  91.4 us (31%)
  starting transfers between devices  66.8 us (23%)
  local copies, waits for them, and re-layouts  17.1 us (6%)
  between operations  14.4 us (5%)
  other arithmetic  7.07 us (2%)
    ppermute x31, waiting for transfers between devices, swap(): return lax.ppermute(value, 'expert', [(i, i ^ mask) for i in range(count)])  44.4 us
    reduce_scatter x2, waiting for transfers between devices, line_scatter(): lax.psum_scatter(value, 'expert', scatter_dimension=0, tiled=True, axis_i...  36 us
    ppermute x31, starting transfers between devices, swap(): return lax.ppermute(value, 'expert', [(i, i ^ mask) for i in range(count)])  26.8 us
    all_to_all x4, starting transfers between devices, exchange(): return lax.all_to_all(value, 'expert', 0, 0, tiled=True)  17.2 us
    all_to_all x4, starting transfers between devices, team_exchange(): lax.all_to_all(value, 'expert', 0, 0, tiled=True, axis_index_groups=planes)  16.8 us
    pallas_call x1, Pallas kernels, expert(): pl.pallas_call(functools.partial(expert_kernel, chunk=chunk), in_specs=[h...  16.2 us
    pallas_call x1, Pallas kernels, attend_back(): pl.pallas_call(functools.partial(attend_back_kernel, count=count), in_spe...  13.1 us
    pallas_call x1, Pallas kernels, feed(): pl.pallas_call(functools.partial(feed_kernel, count=count), out_shape=out...  12.3 us
  transfers between devices with their start and end apart: 47, of which 15 were waited for; matrix products, arithmetic and copies ran while one was open for 4% of the time, Pallas kernels for 30%

profile of v2, /device:TPU:0, one launch (start us, length us, event | category | flops | bytes accessed | tf_op | source)
XLA Modules:
  0.0 291.2 jit_solution(6372697858111236854)
XLA Ops:
  7.2 2.0 pack.1
  9.2 5.3 %all-to-all-start = ((bf16[8,32,1024]{2,1,0:T(8,128)(2,1)}), bf16[8,32,1024]{2,1,0:T(8,128)(2,1)S(1)}, u32[]{:S(2)}, u32[]{:S(2)}) async-start(bf16[8,32,1024]{2,1,0:T(8,128)(2,1)} %pack.1), calls=%async_computation | async-start | bytes 1048576 | tf_op jit(solution)/shard_map/all_to_all | solution.py:783
  14.5 1.6 collective-permute-start.2
  16.1 2.6 collective-permute-start.1
  18.7 1.3 collective-permute-start
  20.0 1.4 copy.26.routes_ref
  21.4 2.5 place_rows.1
  25.0 5.2 %all-to-all-start.1 = ((bf16[32,8,1024]{2,1,0:T(8,128)(2,1)}), bf16[32,8,1024]{2,1,0:T(8,128)(2,1)S(1)}, u32[]{:S(2)}, u32[]{:S(2)}) async-start(bf16[32,8,1024]{2,1,0:T(8,128)(2,1)} %bitcast.61), calls=%async_computation.1 | async-start | bytes 1048576 | tf_op jit(solution)/shard_map/all_to_all | solution.py:780
  31.0 1.8 collective-permute-start.3
  32.9 1.5 collective-permute-start.4
  34.6 10.8 %collective-permute-done.3 = bf16[144,1024]{1,0:T(8,128)(2,1)S(1)} collective-permute-done((bf16[144,1024]{1,0:T(8,128)(2,1)S(1)}, bf16[144,1024]{1,0:T(8,128)(2,1)S(1)}, u32[]{:S(2)}, u32[]{:S(2)}) %collective-permute-start.3) | collective-permute-done | bytes 294944 | tf_op jit(solution)/shard_map/ppermute | solution.py:777
  45.6 6.6 %collective-permute-done.5 = bf16[144,1024]{1,0:T(8,128)(2,1)S(1)} collective-permute-done((bf16[144,1024]{1,0:T(8,128)(2,1)S(1)}, bf16[144,1024]{1,0:T(8,128)(2,1)S(1)}, u32[]{:S(2)}, u32[]{:S(2)}) %collective-permute-start.5) | collective-permute-done | bytes 294944 | tf_op jit(solution)/shard_map/ppermute | solution.py:777
  52.9 1.0 collective-permute-start.10
  53.8 1.5 collective-permute-start.9
  55.3 1.1 collective-permute-start.8
  57.8 4.6 %all-gather.4.cloned.1.call-done.got_ref.small_ref = bf16[1024,512]{1,0:T(8,128)(2,1)} async-done(((bf16[256,512]{1,0:T(8,128)(2,1)}), bf16[1024,512]{1,0:T(8,128)(2,1)}) %all-gather.4.cloned.1.call-update) | async-done | bytes 1048592 | tf_op jit(solution)/shard_map/all_gather | solution.py:786
  62.4 7.1 %attend.1 = (bf16[8,128,384]{2,1,0:T(8,128)(2,1)}, bf16[8,128,128]{2,1,0:T(8,128)(2,1)}) custom-call(s32[2]{0:T(128)} %pad_add_fusion.place_ref, bf16[2,144,1024]{2,1,0:T(8,128)(2,1)} %copy-done.27, bf16[2,144,1024]{2,1,0:T(8,128)(2,1)} %copy-done.28, bf16[2,144,1024]{2,1,0:T(8,128)(2,1)} %collective-permute-done.6.f0_ref, ...), custom_call_target="tpu_custom_call" | custom-call | flops 1 | bytes 1 | tf_op jit(solution)/shard_map/attend/pallas_call | solution.py:159
  69.5 1.1 pad_maximum_fusion.near_ref
  70.6 3.8 %all-to-all-start.2 = ((bf16[8,128,128]{2,1,0:T(8,128)(2,1)}), bf16[8,128,128]{2,1,0:T(8,128)(2,1)S(1)}, u32[]{:S(2)}, u32[]{:S(2)}) async-start(bf16[8,128,128]{2,1,0:T(8,128)(2,1)} %get-tuple-element.131), calls=%async_computation.2 | async-start | bytes 524288 | tf_op jit(solution)/shard_map/all_to_all | solution.py:783
  74.4 1.0 copy-done.32
  75.4 3.0 %order.1 = bf16[4,8,32,1024]{3,2,1,0:T(8,128)(2,1)} custom-call(s32[2]{0:T(128)} %pad_add_fusion.place_ref, bf16[4,128,1024]{2,1,0:T(8,128)(2,1)} %copy-done.25, bf16[4,128,1024]{2,1,0:T(8,128)(2,1)} %copy-done.32), custom_call_target="tpu_custom_call" | custom-call | flops 1 | bytes 1 | tf_op jit(solution)/shard_map/order/pallas_call | solution.py:735
  78.4 2.9 all-to-all-done.2.att_ref
  82.0 4.2 %middle.1 = (f32[128,1024]{1,0:T(8,128)}, bf16[128,1024]{1,0:T(8,128)(2,1)}, bf16[128,1024]{1,0:T(8,128)(2,1)}, f32[128,128]{1,0:T(8,128)}, bf16[256,1152]{1,0:T(8,128)(2,1)}) custom-call(bf16[8,128,128]{2,1,0:T(8,128)(2,1)} %copy-done.33, bf16[1024,1024]{1,0:T(8,128)(2,1)} %bitcast.49, bf16[128,1024]{1,0:T(8,128)(2,1)} %x_ref.1, ...), custom_call_target="tpu_custom_call" | custom-call | flops 1 | bytes 1 | tf_op jit(solution)/shard_map/middle/pallas_call | solution.py:336
  86.8 1.4 collective-permute-start.13
  88.2 1.5 collective-permute-start.12
  89.7 2.6 all-to-all-start.3
  92.4 4.2 %collective-permute-done.14 = bf16[128,1024]{1,0:T(8,128)(2,1)S(1)} collective-permute-done((bf16[128,1024]{1,0:T(8,128)(2,1)}, bf16[128,1024]{1,0:T(8,128)(2,1)S(1)}, u32[]{:S(2)}, u32[]{:S(2)}) %collective-permute-start.14) | collective-permute-done | bytes 262176 | tf_op jit(solution)/shard_map/ppermute | solution.py:777
  96.6 7.6 %collective-permute-done.13 = bf16[128,1024]{1,0:T(8,128)(2,1)S(1)} collective-permute-done((bf16[128,1024]{1,0:T(8,128)(2,1)}, bf16[128,1024]{1,0:T(8,128)(2,1)S(1)}, u32[]{:S(2)}, u32[]{:S(2)}) %collective-permute-start.13) | collective-permute-done | bytes 262176 | tf_op jit(solution)/shard_map/ppermute | solution.py:777
  104.2 1.1 pad_maximum_fusion.1.near_ref
  105.5 2.4 collective-permute-start.18
  108.2 0.9 collective-permute-start.16
  109.9 16.2 %expert.1 = (bf16[256,4096]{1,0:T(8,128)(2,1)}, bf16[256,4096]{1,0:T(8,128)(2,1)}, bf16[256,2048]{1,0:T(8,128)(2,1)}, bf16[256,1024]{1,0:T(8,128)(2,1)}) custom-call(bf16[256,1152]{1,0:T(8,128)(2,1)} %bitcast.51, bf16[256,1024]{1,0:T(8,128)(2,1)} %bitcast.54, bf16[1,1024,4096]{2,1,0:T(8,128)(2,1)} %widen_hbm.1, bf16[1,4096,1024]{2,1,0:T(8,128)(2,1)} %narrow_hbm.1), custom_call_target="tpu_custom_call" | custom-call | flops 1 | bytes 1 | tf_op jit(solution)/shard_map/expert/pallas_call | solution.py:400
  126.2 6.0 %collective-permute-done.17 = bf16[256,1024]{1,0:T(8,128)(2,1)} collective-permute-done((bf16[256,1024]{1,0:T(8,128)(2,1)S(1)}, bf16[256,1024]{1,0:T(8,128)(2,1)}, u32[]{:S(2)}, u32[]{:S(2)}) %collective-permute-start.17) | collective-permute-done | bytes 524320 | tf_op jit(solution)/shard_map/ppermute | solution.py:777
  132.1 1.9 slice_bitcast_fusion.2
  134.0 1.9 slice_bitcast_fusion
  136.2 3.8 %all-to-all-start.4 = ((bf16[32,8,2048]{2,1,0:T(8,128)(2,1)}), bf16[32,8,2048]{2,1,0:T(8,128)(2,1)S(1)}, u32[]{:S(2)}, u32[]{:S(2)}) async-start(bf16[32,8,2048]{2,1,0:T(8,128)(2,1)} %bitcast.58), calls=%async_computation.4 | async-start | bytes 2097152 | tf_op jit(solution)/shard_map/all_to_all | solution.py:780
  140.2 0.9 copy-done.31
  141.1 12.3 %feed.1 = (f32[4,128,1152]{2,1,0:T(8,128)}, bf16[4,128,512]{2,1,0:T(8,128)(2,1)}, bf16[4,128,640]{2,1,0:T(8,128)(2,1)}, f32[4,128,1024]{2,1,0:T(8,128)}, bf16[4,...) custom-call(bf16[4,128,1024]{2,1,0:T(8,128)(2,1)} %copy-done.23, ...), custom_call_target="tpu_custom_call" | custom-call | flops 1 | bytes 1 | tf_op jit(solution)/shard_map/feed/pallas_call | solution.py:520
  154.1 2.5 collective-permute-done.21.refs_0_
  156.6 1.7 copy-done.1
  158.5 0.8 copy-done.8
  159.6 2.2 pad_maximum_fusion.2.near_att
  162.1 1.8 collective-permute-start.23
  163.9 1.5 collective-permute-start.24
  165.6 9.7 %widen_grads.1 = f32[1,1024,4096]{2,1,0:T(8,128)} custom-call(bf16[256,1152]{1,0:T(8,128)(2,1)} %bitcast.52, bf16[256,4096]{1,0:T(8,128)(2,1)} %get-tuple-element.169.d_ref), custom_call_target="tpu_custom_call" | custom-call | flops 1 | bytes 1 | tf_op jit(solution)/shard_map/widen_grads/pallas_call | solution.py:453
  175.3 3.8 %collective-permute-done.24.r2_ref = bf16[128,1152]{1,0:T(8,128)(2,1)} collective-permute-done((bf16[128,1152]{1,0:T(8,128)(2,1)S(1)}, bf16[128,1152]{1,0:T(8,128)(2,1)}, u32[]{:S(2)}, u32[]{:S(2)}) %collective-permute-start.24) | collective-permute-done | bytes 294944 | tf_op jit(solution)/shard_map/ppermute | solution.py:777
  179.2 5.8 %after.1 = (f32[128,1024]{1,0:T(8,128)}, f32[128,1024]{1,0:T(8,128)}, f32[1024,128]{1,0:T(8,128)}, bf16[8,256,128]{2,1,0:T(8,128)(2,1)}) custom-call(f32[128,1152]{1,0:T(8,128)} %copy-done.8, bf16[128,1152]{1,0:T(8,128)(2,1)} %copy-done.34, bf16[128,1152]{1,0:T(8,128)(2,1)} %collective-permute-done.24.r2_ref, ...), custom_call_target="tpu_custom_call" | custom-call | flops 1 | bytes 1 | tf_op jit(solution)/shard_map/after/pallas_call | solution.py:616
  185.0 4.2 %all-to-all-start.5 = ((bf16[8,256,128]{2,1,0:T(8,128)(2,1)}), bf16[8,256,128]{2,1,0:T(8,128)(2,1)}, u32[]{:S(2)}, u32[]{:S(2)}) async-start(bf16[8,256,128]{2,1,0:T(8,128)(2,1)} %get-tuple-element.175), calls=%async_computation.5 | async-start | bytes 1048576 | tf_op jit(solution)/shard_map/all_to_all | solution.py:783
  189.2 1.1 halve.4
  191.1 1.9 collective-permute-start.27
  193.0 1.5 collective-permute-start.28
  194.6 4.8 %all-to-all-done.5.d_ref = bf16[8,256,128]{2,1,0:T(8,128)(2,1)} async-done(((bf16[8,256,128]{2,1,0:T(8,128)(2,1)}), bf16[8,256,128]{2,1,0:T(8,128)(2,1)}, u32[]{:S(2)}, u32[]{:S(2)}) %all-to-all-start.5) | async-done | bytes 524320 | tf_op jit(solution)/shard_map/all_to_all | solution.py:783
  199.4 3.6 %all-to-all-start.6 = ((bf16[8,32,512]{2,1,0:T(8,128)(2,1)}), bf16[8,32,512]{2,1,0:T(8,128)(2,1)S(1)}, u32[]{:S(2)}, u32[]{:S(2)}) async-start(bf16[8,32,512]{2,1,0:T(8,128)(2,1)} %bitcast.66), calls=%async_computation.7 | async-start | bytes 524288 | tf_op jit(solution)/shard_map/all_to_all | solution.py:783
  203.0 13.1 %attend_back.1 = (f32[4,128,1024]{2,1,0:T(8,128)}, bf16[4,128,1024]{2,1,0:T(8,128)(2,1)}, bf16[1024,640]{1,0:T(8,128)(2,1)}) custom-call(s32[2]{0:T(128)} %pad_add_fusion.place_ref, bf16[2,144,1024]{2,1,0:T(8,128)(2,1)} %copy-done.27, bf16[2,144,1024]{2,1,0:T(8,128)(2,1)} %copy-done.28, bf16[2,144,1024]{2,1,0:T(8,128)(2,1)} %collective-permute-done.6.f0_ref, ...), custom_call_target="tpu_custom_call" | custom-call | flops 20000000000 | bytes 1 | tf_op jit(solution)/shard_map/attend_back/pallas_call | solution.py:242
  219.1 5.7 %all-to-all-start.7 = ((bf16[32,32,640]{2,1,0:T(8,128)(2,1)}), bf16[32,32,640]{2,1,0:T(8,128)(2,1)S(1)}, u32[]{:S(2)}, u32[]{:S(2)}) async-start(bf16[32,32,640]{2,1,0:T(8,128)(2,1)} %bitcast.57), calls=%async_computation.8 | async-start | bytes 2621440 | tf_op jit(solution)/shard_map/all_to_all | solution.py:780
  225.7 2.6 collective-permute-done.30.refs_0_
  228.3 1.1 halve.5
  230.2 1.8 collective-permute-start.31
  231.9 1.5 collective-permute-start.32
  233.7 36.0 %reduce-scatter.5.cloned.1.call-done = bf16[128,1024]{1,0:T(8,128)(2,1)} async-done(((bf16[512,1024]{1,0:T(8,128)(2,1)}), bf16[128,1024]{1,0:T(8,128)(2,1)}) %reduce-scatter.5.cloned.1.call-update) | async-done | bytes 262160 | tf_op jit(solution)/shard_map/reduce_scatter | solution.py:789
  269.7 1.8 convert_element_type.9
  271.6 9.6 %narrow_grads.1 = f32[1,4096,1024]{2,1,0:T(8,128)} custom-call(bf16[256,1024]{1,0:T(8,128)(2,1)} %get-tuple-element.205.rows_ref, bf16[256,4096]{1,0:T(8,128)(2,1)} %get-tuple-element.206.act_ref), custom_call_target="tpu_custom_call" | custom-call | flops 1 | bytes 1 | tf_op jit(solution)/shard_map/narrow_grads/pallas_call | solution.py:431
  281.3 2.2 last.1
  283.5 1.2 owner_sums.1
  (148 shorter events, 15.0 us)
Async XLA Ops:
  7.2 23.8 %copy-start.37 = (s32[1,128]{1,0:T(1,128)S(1)}, s32[1,128]{1,0:T(1,128)}, u32[]{:S(2)}) copy-start(s32[1,128]{1,0:T(1,128)} %param.26) | copy-start | bytes 1540
  7.2 23.8 %copy-start.2 = (bf16[128,1024]{1,0:T(8,128)(2,1)S(1)}, bf16[128,1024]{1,0:T(8,128)(2,1)}, u32[]{:S(2)}) copy-start(bf16[128,1024]{1,0:T(8,128)(2,1)} %x_ref.1) | copy-start | bytes 786436
  9.2 25.4 %copy-start.36 = (bf16[32,1024]{1,0:T(8,128)(2,1)S(1)}, bf16[32,1024]{1,0:T(8,128)(2,1)}, u32[]{:S(2)}) copy-start(bf16[32,1024]{1,0:T(8,128)(2,1)} %param.17) | copy-start | bytes 196612
  9.2 15.0 %all-to-all-start = ((bf16[8,32,1024]{2,1,0:T(8,128)(2,1)}), bf16[8,32,1024]{2,1,0:T(8,128)(2,1)S(1)}, u32[]{:S(2)}, u32[]{:S(2)}) async-start(bf16[8,32,1024]{2,1,0:T(8,128)(2,1)} %pack.1), calls=%async_computation | async-start | bytes 1048576 | tf_op jit(solution)/shard_map/all_to_all | solution.py:783
  14.5 9.4 %collective-permute-start.2 = (bf16[32,1024]{1,0:T(8,128)(2,1)}, bf16[32,1024]{1,0:T(8,128)(2,1)S(1)}, u32[]{:S(2)}, u32[]{:S(2)}) collective-permute-start(bf16[32,1024]{1,0:T(8,128)(2,1)} %param.17), channel_id=1, source_target_pairs={{24,0},{25,1},{26,2},{27,3},{28,4},{29,5},{30,6},{31,7},{0,8},{1,9... | collective-permute-start | bytes 196616 | tf_op jit(solution)/shard_map/ppermute | solution.py:830
  16.1 7.9 %collective-permute-start.1 = (bf16[32,1024]{1,0:T(8,128)(2,1)}, bf16[32,1024]{1,0:T(8,128)(2,1)S(1)}, u32[]{:S(2)}, u32[]{:S(2)}) collective-permute-start(bf16[32,1024]{1,0:T(8,128)(2,1)} %param.17), channel_id=1, source_target_pairs={{16,0},{17,1},{18,2},{19,3},{20,4},{21,5},{22,6},{23,7},{24,8},{25... | collective-permute-start | bytes 196616 | tf_op jit(solution)/shard_map/ppermute | solution.py:830
  18.7 5.6 %collective-permute-start = (bf16[32,1024]{1,0:T(8,128)(2,1)}, bf16[32,1024]{1,0:T(8,128)(2,1)S(1)}, u32[]{:S(2)}, u32[]{:S(2)}) collective-permute-start(bf16[32,1024]{1,0:T(8,128)(2,1)} %param.17), channel_id=1, source_target_pairs={{8,0},{9,1},{10,2},{11,3},{12,4},{13,5},{14,6},{15,7},{16,8},{17,9... | collective-permute-start | bytes 196616 | tf_op jit(solution)/shard_map/ppermute | solution.py:830
  25.0 27.3 %all-to-all-start.1 = ((bf16[32,8,1024]{2,1,0:T(8,128)(2,1)}), bf16[32,8,1024]{2,1,0:T(8,128)(2,1)S(1)}, u32[]{:S(2)}, u32[]{:S(2)}) async-start(bf16[32,8,1024]{2,1,0:T(8,128)(2,1)} %bitcast.61), calls=%async_computation.1 | async-start | bytes 1048576 | tf_op jit(solution)/shard_map/all_to_all | solution.py:780
  30.2 32.2 %all-gather.4.cloned.1.call-start = ((), (), s32[]{:S(2)}) async-start(), calls=%async_computation.10 | async-start | bytes 1310720 | tf_op jit(solution)/shard_map/all_gather | solution.py:786
  30.9 74.5 %all-gather.6.cloned.1.call-start = ((), (), s32[]{:S(2)}) async-start(), calls=%async_computation.11 | async-start | bytes 1310720 | tf_op jit(solution)/shard_map/all_gather | solution.py:786
  31.0 14.3 %collective-permute-start.3 = (bf16[144,1024]{1,0:T(8,128)(2,1)S(1)}, bf16[144,1024]{1,0:T(8,128)(2,1)S(1)}, u32[]{:S(2)}, u32[]{:S(2)}) collective-permute-start(bf16[144,1024]{1,0:T(8,128)(2,1)S(1)} %get-tuple-element.229), channel_id=1, source_target_pairs={{0,2},{1,3},{2,0},{3,1},{4,6},{5,7},{6,4},{7,5},{8,10},{9,11},{10,... | collective-permute-start | bytes 884744 | tf_op jit(solution)/shard_map/ppermute | solution.py:777
  32.9 12.7 %collective-permute-start.4 = (bf16[144,1024]{1,0:T(8,128)(2,1)S(1)}, bf16[144,1024]{1,0:T(8,128)(2,1)S(1)}, u32[]{:S(2)}, u32[]{:S(2)}) collective-permute-start(bf16[144,1024]{1,0:T(8,128)(2,1)S(1)} %get-tuple-element.229), channel_id=1, source_target_pairs={{0,4},{1,5},{2,6},{3,7},{4,0},{5,1},{6,2},{7,3},{8,12},{9,13},{10,... | collective-permute-start | bytes 884744 | tf_op jit(solution)/shard_map/ppermute | solution.py:777
  34.3 17.8 %collective-permute-start.5 = (bf16[144,1024]{1,0:T(8,128)(2,1)S(1)}, bf16[144,1024]{1,0:T(8,128)(2,1)S(1)}, u32[]{:S(2)}, u32[]{:S(2)}) collective-permute-start(bf16[144,1024]{1,0:T(8,128)(2,1)S(1)} %get-tuple-element.229), channel_id=1, source_target_pairs={{0,6},{1,7},{2,4},{3,5},{4,2},{5,3},{6,0},{7,1},{8,14},{9,15},{10,... | collective-permute-start | bytes 884744 | tf_op jit(solution)/shard_map/ppermute | solution.py:777
  45.4 16.9 %copy-start.27 = (bf16[2,144,1024]{2,1,0:T(8,128)(2,1)}, bf16[2,144,1024]{2,1,0:T(8,128)(2,1)S(1)}, u32[]{:S(2)}) copy-start(bf16[2,144,1024]{2,1,0:T(8,128)(2,1)S(1)} %pad_maximum_fusion.4.n0_ref) | copy-start | bytes 1769476
  52.2 10.1 %copy-start.28 = (bf16[2,144,1024]{2,1,0:T(8,128)(2,1)}, bf16[2,144,1024]{2,1,0:T(8,128)(2,1)S(1)}, u32[]{:S(2)}) copy-start(bf16[2,144,1024]{2,1,0:T(8,128)(2,1)S(1)} %pad_maximum_fusion.5.n1_ref) | copy-start | bytes 1769476
  52.3 17.2 %copy-start.30 = (bf16[32,8,1024]{2,1,0:T(8,128)(2,1)}, bf16[32,8,1024]{2,1,0:T(8,128)(2,1)S(1)}, u32[]{:S(2)}) copy-start(bf16[32,8,1024]{2,1,0:T(8,128)(2,1)S(1)} %all-to-all-done.1) | copy-start | bytes 1572868
  52.3 10.1 %collective-permute-start.6 = (bf16[2,144,1024]{2,1,0:T(8,128)(2,1)S(1)}, bf16[2,144,1024]{2,1,0:T(8,128)(2,1)}, u32[]{:S(2)}, u32[]{:S(2)}) collective-permute-start(bf16[2,144,1024]{2,1,0:T(8,128)(2,1)S(1)} %pad_maximum_fusion.4.n0_ref), channel_id=1, source_target_pairs={{0,1},{1,0},{2,3},{3,2},{4,5},{5,4},{6,7},{7,6},{8,9},{9,8},{10,11... | collective-permute-start | bytes 1769480 | tf_op jit(solution)/shard_map/ppermute | solution.py:777
  52.3 10.0 %collective-permute-start.7 = (bf16[2,144,1024]{2,1,0:T(8,128)(2,1)S(1)}, bf16[2,144,1024]{2,1,0:T(8,128)(2,1)}, u32[]{:S(2)}, u32[]{:S(2)}) collective-permute-start(bf16[2,144,1024]{2,1,0:T(8,128)(2,1)S(1)} %pad_maximum_fusion.5.n1_ref), channel_id=1, source_target_pairs={{0,1},{1,0},{2,3},{3,2},{4,5},{5,4},{6,7},{7,6},{8,9},{9,8},{10,11... | collective-permute-start | bytes 1769480 | tf_op jit(solution)/shard_map/ppermute | solution.py:777
  52.9 16.6 %collective-permute-start.10 = (bf16[128,1024]{1,0:T(8,128)(2,1)S(1)}, bf16[128,1024]{1,0:T(8,128)(2,1)S(1)}, u32[]{:S(2)}, u32[]{:S(2)}) collective-permute-start(bf16[128,1024]{1,0:T(8,128)(2,1)S(1)} %constant_dynamic-update-slice_fusion), channel_id=1, source_target_pairs={{0,6},{1,7},{2,4},{3,5},{4,2},{5,3},{6,0},{7,1},{8,14},{9,15},{10,... | collective-permute-start | bytes 786440 | tf_op jit(solution)/shard_map/ppermute | solution.py:777
  53.8 15.6 %collective-permute-start.9 = (bf16[128,1024]{1,0:T(8,128)(2,1)S(1)}, bf16[128,1024]{1,0:T(8,128)(2,1)S(1)}, u32[]{:S(2)}, u32[]{:S(2)}) collective-permute-start(bf16[128,1024]{1,0:T(8,128)(2,1)S(1)} %constant_dynamic-update-slice_fusion), channel_id=1, source_target_pairs={{0,4},{1,5},{2,6},{3,7},{4,0},{5,1},{6,2},{7,3},{8,12},{9,13},{10,... | collective-permute-start | bytes 786440 | tf_op jit(solution)/shard_map/ppermute | solution.py:777
  55.3 14.1 %collective-permute-start.8 = (bf16[128,1024]{1,0:T(8,128)(2,1)S(1)}, bf16[128,1024]{1,0:T(8,128)(2,1)}, u32[]{:S(2)}, u32[]{:S(2)}) collective-permute-start(bf16[128,1024]{1,0:T(8,128)(2,1)S(1)} %constant_dynamic-update-slice_fusion), channel_id=1, source_target_pairs={{0,2},{1,3},{2,0},{3,1},{4,6},{5,7},{6,4},{7,5},{8,10},{9,11},{10,... | collective-permute-start | bytes 786440 | tf_op jit(solution)/shard_map/ppermute | solution.py:777
  70.6 3.8 %collective-permute-start.11 = (bf16[4,128,1024]{2,1,0:T(8,128)(2,1)S(1)}, bf16[4,128,1024]{2,1,0:T(8,128)(2,1)S(1)}, u32[]{:S(2)}, u32[]{:S(2)}) collective-permute-start(bf16[4,128,1024]{2,1,0:T(8,128)(2,1)S(1)} %pad_maximum_fusion.near_ref), channel_id=1, source_target_pairs={{0,1},{1,0},{2,3},{3,2},{4,5},{5,4},{6,7},{7,6},{8,9},{9,8},{10,11... | collective-permute-start | bytes 3145736 | tf_op jit(solution)/shard_map/ppermute | solution.py:777
  70.6 10.7 %all-to-all-start.2 = ((bf16[8,128,128]{2,1,0:T(8,128)(2,1)}), bf16[8,128,128]{2,1,0:T(8,128)(2,1)S(1)}, u32[]{:S(2)}, u32[]{:S(2)}) async-start(bf16[8,128,128]{2,1,0:T(8,128)(2,1)} %get-tuple-element.131), calls=%async_computation.2 | async-start | bytes 524288 | tf_op jit(solution)/shard_map/all_to_all | solution.py:783
  86.2 19.2 %copy-start.35 = (bf16[128,1024]{1,0:T(8,128)(2,1)S(1)}, bf16[128,1024]{1,0:T(8,128)(2,1)}, u32[]{:S(2)}) copy-start(bf16[128,1024]{1,0:T(8,128)(2,1)} %get-tuple-element.147) | copy-start | bytes 786436
  86.2 19.3 %copy-start.29 = (bf16[128,1024]{1,0:T(8,128)(2,1)S(1)}, bf16[128,1024]{1,0:T(8,128)(2,1)}, u32[]{:S(2)}) copy-start(bf16[128,1024]{1,0:T(8,128)(2,1)} %g_ref.3) | copy-start | bytes 786436
  86.2 10.4 %collective-permute-start.14 = (bf16[128,1024]{1,0:T(8,128)(2,1)}, bf16[128,1024]{1,0:T(8,128)(2,1)S(1)}, u32[]{:S(2)}, u32[]{:S(2)}) collective-permute-start(bf16[128,1024]{1,0:T(8,128)(2,1)} %get-tuple-element.138.second_ref), channel_id=1, source_target_pairs={{0,6},{1,7},{2,4},{3,5},{4,2},{5,3},{6,0},{7,1},{8,14},{9,15},{10,... | collective-permute-start | bytes 786440 | tf_op jit(solution)/shard_map/ppermute | solution.py:777
  86.8 17.5 %collective-permute-start.13 = (bf16[128,1024]{1,0:T(8,128)(2,1)}, bf16[128,1024]{1,0:T(8,128)(2,1)S(1)}, u32[]{:S(2)}, u32[]{:S(2)}) collective-permute-start(bf16[128,1024]{1,0:T(8,128)(2,1)} %get-tuple-element.138.second_ref), channel_id=1, source_target_pairs={{0,4},{1,5},{2,6},{3,7},{4,0},{5,1},{6,2},{7,3},{8,12},{9,13},{10,... | collective-permute-start | bytes 786440 | tf_op jit(solution)/shard_map/ppermute | solution.py:777
  88.2 16.0 %collective-permute-start.12 = (bf16[128,1024]{1,0:T(8,128)(2,1)}, bf16[128,1024]{1,0:T(8,128)(2,1)S(1)}, u32[]{:S(2)}, u32[]{:S(2)}) collective-permute-start(bf16[128,1024]{1,0:T(8,128)(2,1)} %get-tuple-element.138.second_ref), channel_id=1, source_target_pairs={{0,2},{1,3},{2,0},{3,1},{4,6},{5,7},{6,4},{7,5},{8,10},{9,11},{10,... | collective-permute-start | bytes 786440 | tf_op jit(solution)/shard_map/ppermute | solution.py:777
  89.7 19.4 %all-to-all-start.3 = ((bf16[32,8,1152]{2,1,0:T(8,128)(2,1)}), bf16[32,8,1152]{2,1,0:T(8,128)(2,1)S(1)}, u32[]{:S(2)}, u32[]{:S(2)}) async-start(bf16[32,8,1152]{2,1,0:T(8,128)(2,1)} %bitcast.60), calls=%async_computation.3 | async-start | bytes 1179648 | tf_op jit(solution)/shard_map/all_to_all | solution.py:780
  92.3 47.9 %all-gather.8.cloned.1.call-start = ((), (), s32[]{:S(2)}) async-start(), calls=%async_computation.12 | async-start | bytes 1310720 | tf_op jit(solution)/shard_map/all_gather | solution.py:786
  105.3 20.8 %copy-start.23 = (bf16[4,128,1024]{2,1,0:T(8,128)(2,1)}, bf16[4,128,1024]{2,1,0:T(8,128)(2,1)S(1)}, u32[]{:S(2)}) copy-start(bf16[4,128,1024]{2,1,0:T(8,128)(2,1)S(1)} %pad_maximum_fusion.1.near_ref) | copy-start | bytes 3145732
  105.4 3.7 %collective-permute-start.15 = (bf16[4,128,1024]{2,1,0:T(8,128)(2,1)S(1)}, bf16[4,128,1024]{2,1,0:T(8,128)(2,1)}, u32[]{:S(2)}, u32[]{:S(2)}) collective-permute-start(bf16[4,128,1024]{2,1,0:T(8,128)(2,1)S(1)} %pad_maximum_fusion.1.near_ref), channel_id=1, source_target_pairs={{0,1},{1,0},{2,3},{3,2},{4,5},{5,4},{6,7},{7,6},{8,9},{9,8},{10,11... | collective-permute-start | bytes 3145736 | tf_op jit(solution)/shard_map/ppermute | solution.py:777
  105.5 20.6 %collective-permute-start.18 = (bf16[256,1024]{1,0:T(8,128)(2,1)S(1)}, bf16[256,1024]{1,0:T(8,128)(2,1)S(1)}, u32[]{:S(2)}, u32[]{:S(2)}) collective-permute-start(bf16[256,1024]{1,0:T(8,128)(2,1)S(1)} %constant_dynamic-update-slice_fusion.4), channel_id=1, source_target_pairs={{0,6},{1,7},{2,4},{3,5},{4,2},{5,3},{6,0},{7,1},{8,14},{9,15},{10,... | collective-permute-start | bytes 1572872 | tf_op jit(solution)/shard_map/ppermute | solution.py:777
  107.9 24.3 %collective-permute-start.17 = (bf16[256,1024]{1,0:T(8,128)(2,1)S(1)}, bf16[256,1024]{1,0:T(8,128)(2,1)}, u32[]{:S(2)}, u32[]{:S(2)}) collective-permute-start(bf16[256,1024]{1,0:T(8,128)(2,1)S(1)} %constant_dynamic-update-slice_fusion.4), channel_id=1, source_target_pairs={{0,4},{1,5},{2,6},{3,7},{4,0},{5,1},{6,2},{7,3},{8,12},{9,13},{10,... | collective-permute-start | bytes 1572872 | tf_op jit(solution)/shard_map/ppermute | solution.py:777
  108.2 23.9 %collective-permute-start.16 = (bf16[256,1024]{1,0:T(8,128)(2,1)S(1)}, bf16[256,1024]{1,0:T(8,128)(2,1)}, u32[]{:S(2)}, u32[]{:S(2)}) collective-permute-start(bf16[256,1024]{1,0:T(8,128)(2,1)S(1)} %constant_dynamic-update-slice_fusion.4), channel_id=1, source_target_pairs={{0,2},{1,3},{2,0},{3,1},{4,6},{5,7},{6,4},{7,5},{8,10},{9,11},{10,... | collective-permute-start | bytes 1572872 | tf_op jit(solution)/shard_map/ppermute | solution.py:777
  136.1 4.1 %collective-permute-start.20 = (bf16[4,128,1024]{2,1,0:T(8,128)(2,1)S(1)}, bf16[4,128,1024]{2,1,0:T(8,128)(2,1)S(1)}, u32[]{:S(2)}, u32[]{:S(2)}) collective-permute-start(bf16[4,128,1024]{2,1,0:T(8,128)(2,1)S(1)} %pad_maximum_fusion.3.g_near_ref), channel_id=1, source_target_pairs={{0,1},{1,0},{2,3},{3,2},{4,5},{5,4},{6,7},{7,6},{8,9},{9,8},{10,11... | collective-permute-start | bytes 3145736 | tf_op jit(solution)/shard_map/ppermute | solution.py:777
  136.2 39.1 %all-to-all-start.4 = ((bf16[32,8,2048]{2,1,0:T(8,128)(2,1)}), bf16[32,8,2048]{2,1,0:T(8,128)(2,1)S(1)}, u32[]{:S(2)}, u32[]{:S(2)}) async-start(bf16[32,8,2048]{2,1,0:T(8,128)(2,1)} %bitcast.58), calls=%async_computation.4 | async-start | bytes 2097152 | tf_op jit(solution)/shard_map/all_to_all | solution.py:780
  139.9 59.5 %reduce-scatter.3.cloned.1.call-start = ((), (), s32[]{:S(2)}) async-start(), calls=%async_computation.13 | async-start | bytes 1310720 | tf_op jit(solution)/shard_map/reduce_scatter | solution.py:789
  153.5 3.1 %collective-permute-start.22 = (bf16[4,128,640]{2,1,0:T(8,128)(2,1)}, bf16[4,128,640]{2,1,0:T(8,128)(2,1)S(1)}, u32[]{:S(2)}, u32[]{:S(2)}) collective-permute-start(bf16[4,128,640]{2,1,0:T(8,128)(2,1)} %get-tuple-element.159), channel_id=1, source_target_pairs={{0,1},{1,0},{2,3},{3,2},{4,5},{5,4},{6,7},{7,6},{8,9},{9,8},{10,11... | collective-permute-start | bytes 1966088 | tf_op jit(solution)/shard_map/ppermute | solution.py:777
  153.8 2.8 collective-permute-start.21
  159.4 29.8 %collective-permute-start.26 = (bf16[4,128,1024]{2,1,0:T(8,128)(2,1)}, bf16[4,128,1024]{2,1,0:T(8,128)(2,1)S(1)}, u32[]{:S(2)}, u32[]{:S(2)}) collective-permute-start(bf16[4,128,1024]{2,1,0:T(8,128)(2,1)} %get-tuple-element.185), channel_id=1, source_target_pairs={{0,1},{1,0},{2,3},{3,2},{4,5},{5,4},{6,7},{7,6},{8,9},{9,8},{10,11... | collective-permute-start | bytes 3145736 | tf_op jit(solution)/shard_map/ppermute | solution.py:777
  161.8 41.2 %collective-permute-start.19 = (bf16[4,128,1024]{2,1,0:T(8,128)(2,1)}, bf16[4,128,1024]{2,1,0:T(8,128)(2,1)}, u32[]{:S(2)}, u32[]{:S(2)}) collective-permute-start(bf16[4,128,1024]{2,1,0:T(8,128)(2,1)} %pad_maximum_fusion.2.near_att), channel_id=1, source_target_pairs={{0,1},{1,0},{2,3},{3,2},{4,5},{5,4},{6,7},{7,6},{8,9},{9,8},{10,11... | collective-permute-start | bytes 3145736 | tf_op jit(solution)/shard_map/ppermute | solution.py:777
  162.1 13.2 %collective-permute-start.23 = (bf16[128,1152]{1,0:T(8,128)(2,1)S(1)}, bf16[128,1152]{1,0:T(8,128)(2,1)S(1)}, u32[]{:S(2)}, u32[]{:S(2)}) collective-permute-start(bf16[128,1152]{1,0:T(8,128)(2,1)S(1)} %get-tuple-element.165), channel_id=1, source_target_pairs={{0,2},{1,3},{2,0},{3,1},{4,6},{5,7},{6,4},{7,5},{8,10},{9,11},{10,... | collective-permute-start | bytes 884744 | tf_op jit(solution)/shard_map/ppermute | solution.py:777
  163.9 15.3 %collective-permute-start.24 = (bf16[128,1152]{1,0:T(8,128)(2,1)S(1)}, bf16[128,1152]{1,0:T(8,128)(2,1)}, u32[]{:S(2)}, u32[]{:S(2)}) collective-permute-start(bf16[128,1152]{1,0:T(8,128)(2,1)S(1)} %get-tuple-element.166), channel_id=1, source_target_pairs={{0,4},{1,5},{2,6},{3,7},{4,0},{5,1},{6,2},{7,3},{8,12},{9,13},{10,... | collective-permute-start | bytes 884744 | tf_op jit(solution)/shard_map/ppermute | solution.py:777
  165.3 13.8 %collective-permute-start.25 = (bf16[128,1152]{1,0:T(8,128)(2,1)S(1)}, bf16[128,1152]{1,0:T(8,128)(2,1)}, u32[]{:S(2)}, u32[]{:S(2)}) collective-permute-start(bf16[128,1152]{1,0:T(8,128)(2,1)S(1)} %get-tuple-element.167), channel_id=1, source_target_pairs={{0,6},{1,7},{2,4},{3,5},{4,2},{5,3},{6,0},{7,1},{8,14},{9,15},{10,... | collective-permute-start | bytes 884744 | tf_op jit(solution)/shard_map/ppermute | solution.py:777
  179.2 10.0 %copy-start.4 = (f32[4,128,1024]{2,1,0:T(8,128)S(1)}, f32[4,128,1024]{2,1,0:T(8,128)}, u32[]{:S(2)}) copy-start(f32[4,128,1024]{2,1,0:T(8,128)} %get-tuple-element.184.keep_ref) | copy-start | bytes 6291460
  185.0 14.4 %all-to-all-start.5 = ((bf16[8,256,128]{2,1,0:T(8,128)(2,1)}), bf16[8,256,128]{2,1,0:T(8,128)(2,1)}, u32[]{:S(2)}, u32[]{:S(2)}) async-start(bf16[8,256,128]{2,1,0:T(8,128)(2,1)} %get-tuple-element.175), calls=%async_computation.5 | async-start | bytes 1048576 | tf_op jit(solution)/shard_map/all_to_all | solution.py:783
  191.1 25.1 %collective-permute-start.27 = (bf16[128,1024]{1,0:T(8,128)(2,1)}, bf16[128,1024]{1,0:T(8,128)(2,1)S(1)}, u32[]{:S(2)}, u32[]{:S(2)}) collective-permute-start(bf16[128,1024]{1,0:T(8,128)(2,1)} %get-tuple-element.186), channel_id=1, source_target_pairs={{0,2},{1,3},{2,0},{3,1},{4,6},{5,7},{6,4},{7,5},{8,10},{9,11},{10,... | collective-permute-start | bytes 786440 | tf_op jit(solution)/shard_map/ppermute | solution.py:777
  193.0 23.9 %collective-permute-start.28 = (bf16[128,1024]{1,0:T(8,128)(2,1)}, bf16[128,1024]{1,0:T(8,128)(2,1)S(1)}, u32[]{:S(2)}, u32[]{:S(2)}) collective-permute-start(bf16[128,1024]{1,0:T(8,128)(2,1)} %get-tuple-element.187), channel_id=1, source_target_pairs={{0,4},{1,5},{2,6},{3,7},{4,0},{5,1},{6,2},{7,3},{8,12},{9,13},{10,... | collective-permute-start | bytes 786440 | tf_op jit(solution)/shard_map/ppermute | solution.py:777
  194.5 23.2 %collective-permute-start.29 = (bf16[128,1024]{1,0:T(8,128)(2,1)}, bf16[128,1024]{1,0:T(8,128)(2,1)S(1)}, u32[]{:S(2)}, u32[]{:S(2)}) collective-permute-start(bf16[128,1024]{1,0:T(8,128)(2,1)} %get-tuple-element.188), channel_id=1, source_target_pairs={{0,6},{1,7},{2,4},{3,5},{4,2},{5,3},{6,0},{7,1},{8,14},{9,15},{10,... | collective-permute-start | bytes 786440 | tf_op jit(solution)/shard_map/ppermute | solution.py:777
  199.4 19.0 %all-to-all-start.6 = ((bf16[8,32,512]{2,1,0:T(8,128)(2,1)}), bf16[8,32,512]{2,1,0:T(8,128)(2,1)S(1)}, u32[]{:S(2)}, u32[]{:S(2)}) async-start(bf16[8,32,512]{2,1,0:T(8,128)(2,1)} %bitcast.66), calls=%async_computation.7 | async-start | bytes 524288 | tf_op jit(solution)/shard_map/all_to_all | solution.py:783
  216.2 12.1 %copy-start.5 = (f32[4,128,1024]{2,1,0:T(8,128)S(1)}, f32[4,128,1024]{2,1,0:T(8,128)}, u32[]{:S(2)}) copy-start(f32[4,128,1024]{2,1,0:T(8,128)} %get-tuple-element.179.keep_ref) | copy-start | bytes 6291460
  219.1 64.4 %all-to-all-start.7 = ((bf16[32,32,640]{2,1,0:T(8,128)(2,1)}), bf16[32,32,640]{2,1,0:T(8,128)(2,1)S(1)}, u32[]{:S(2)}, u32[]{:S(2)}) async-start(bf16[32,32,640]{2,1,0:T(8,128)(2,1)} %bitcast.57), calls=%async_computation.8 | async-start | bytes 2621440 | tf_op jit(solution)/shard_map/all_to_all | solution.py:780
  224.8 44.9 %reduce-scatter.5.cloned.1.call-start = ((), (), s32[]{:S(2)}) async-start(), calls=%async_computation.14 | async-start | bytes 1310720 | tf_op jit(solution)/shard_map/reduce_scatter | solution.py:789
  225.4 2.9 %collective-permute-start.30 = (bf16[4,128,1024]{2,1,0:T(8,128)(2,1)}, bf16[4,128,1024]{2,1,0:T(8,128)(2,1)S(1)}, u32[]{:S(2)}, u32[]{:S(2)}) collective-permute-start(bf16[4,128,1024]{2,1,0:T(8,128)(2,1)} %get-tuple-element.189), channel_id=1, source_target_pairs={{0,1},{1,0},{2,3},{3,2},{4,5},{5,4},{6,7},{7,6},{8,9},{9,8},{10,11... | collective-permute-start | bytes 3145736 | tf_op jit(solution)/shard_map/ppermute | solution.py:777
  230.2 51.0 %collective-permute-start.31 = (bf16[128,1024]{1,0:T(8,128)(2,1)}, bf16[128,1024]{1,0:T(8,128)(2,1)S(1)}, u32[]{:S(2)}, u32[]{:S(2)}) collective-permute-start(bf16[128,1024]{1,0:T(8,128)(2,1)} %get-tuple-element.193), channel_id=1, source_target_pairs={{0,2},{1,3},{2,0},{3,1},{4,6},{5,7},{6,4},{7,5},{8,10},{9,11},{10,... | collective-permute-start | bytes 786440 | tf_op jit(solution)/shard_map/ppermute | solution.py:777
  231.9 49.3 %collective-permute-start.32 = (bf16[128,1024]{1,0:T(8,128)(2,1)}, bf16[128,1024]{1,0:T(8,128)(2,1)S(1)}, u32[]{:S(2)}, u32[]{:S(2)}) collective-permute-start(bf16[128,1024]{1,0:T(8,128)(2,1)} %get-tuple-element.194), channel_id=1, source_target_pairs={{0,4},{1,5},{2,6},{3,7},{4,0},{5,1},{6,2},{7,3},{8,12},{9,13},{10,... | collective-permute-start | bytes 786440 | tf_op jit(solution)/shard_map/ppermute | solution.py:777
  233.4 47.8 %collective-permute-start.33 = (bf16[128,1024]{1,0:T(8,128)(2,1)}, bf16[128,1024]{1,0:T(8,128)(2,1)S(1)}, u32[]{:S(2)}, u32[]{:S(2)}) collective-permute-start(bf16[128,1024]{1,0:T(8,128)(2,1)} %get-tuple-element.195), channel_id=1, source_target_pairs={{0,6},{1,7},{2,4},{3,5},{4,2},{5,3},{6,0},{7,1},{8,14},{9,15},{10,... | collective-permute-start | bytes 786440 | tf_op jit(solution)/shard_map/ppermute | solution.py:777
  271.5 9.7 %copy-start.12 = (f32[128,1024]{1,0:T(8,128)S(1)}, f32[128,1024]{1,0:T(8,128)}, u32[]{:S(2)}) copy-start(f32[128,1024]{1,0:T(8,128)} %copy-done.11) | copy-start | bytes 1572868
  271.5 9.7 %copy-start.14 = (f32[128,1024]{1,0:T(8,128)S(1)}, f32[128,1024]{1,0:T(8,128)}, u32[]{:S(2)}) copy-start(f32[128,1024]{1,0:T(8,128)} %copy-done.13) | copy-start | bytes 1572868
  271.5 9.7 %copy-start.15 = (f32[128,128]{1,0:T(8,128)S(1)}, f32[128,128]{1,0:T(8,128)}, u32[]{:S(2)}) copy-start(f32[128,128]{1,0:T(8,128)} %get-tuple-element.172.stats_ref) | copy-start | bytes 196612
  271.5 9.7 %copy-start.17 = (bf16[128,1024]{1,0:T(8,128)(2,1)S(1)}, bf16[128,1024]{1,0:T(8,128)(2,1)}, u32[]{:S(2)}) copy-start(bf16[128,1024]{1,0:T(8,128)(2,1)} %copy-done.16) | copy-start | bytes 786436
  271.6 9.7 %copy-start.19 = (bf16[128,1024]{1,0:T(8,128)(2,1)S(1)}, bf16[128,1024]{1,0:T(8,128)(2,1)}, u32[]{:S(2)}) copy-start(bf16[128,1024]{1,0:T(8,128)(2,1)} %copy-done.18) | copy-start | bytes 786436
  271.6 9.7 %copy-start.21 = (bf16[128,1024]{1,0:T(8,128)(2,1)S(1)}, bf16[128,1024]{1,0:T(8,128)(2,1)}, u32[]{:S(2)}) copy-start(bf16[128,1024]{1,0:T(8,128)(2,1)} %copy-done.20) | copy-start | bytes 786436
  (21 other events, 67.3 us)
Sparse Core Ops, SparseCore 0:
  33.1 29.1 all-gather.3
  63.9 27.4 all-gather.5
  109.2 27.1 all-gather.7
  153.6 29.5 reduce-scatter.2
  227.7 41.9 reduce-scatter.4
